TPU v7x, 128 devices: a whole 4x4x4 slice. The times are simulated.
128 devices in a mesh: det: 8 (over y, core), tm: 16 (over z, x).
Axes of the slice: x: 4, y: 4, z: 4, core: 2. Of those that a mesh axis runs over, the one named last changes fastest.
Arguments:
- detector_data: float32 [512, 131072], P('det', 'tm'), may hold values from -6 to 6
- sky_map: float32 [4096, 8192], P(('det', 'tm')), may hold values from -6 to 6
- pointing: int32 [512, 1024], P('det', 'tm'), may hold values from 0 to 511
- request_owner: int32 [2048, 1], P(('det', 'tm')), may hold values from 0 to 15; in each aligned block of 16 rows (0 to 15, 16 to 31, ...) at most 2 rows name the same one
- request_block: int32 [2048], P(('det', 'tm')), may hold values from 0 to 63
- beam_kernel: float32 [128, 128], replicated, may hold values from -0.5 to 0.5
- inv_white: float32 [512, 32], P('det'), may hold values from 0.5 to 4
- mode_loading: float32 [512, 16], P('det'), may hold values from -1 to 1
- mode_kernel: float32 [32, 16, 16], replicated, may hold values from -0.75 to 0.75
Outputs:
- map_gradient: float32 [4096, 8192], P(('det', 'tm'))
Inputs may be any that keep to these rules, and one draw needn't show every extreme that they name: `request_owner`: among the 16 requests of one device, no owner is named more than 2 times, and in every draw some device names some owner exactly 2 times.
All inputs are finite; a program needn't handle non-finite values.
Results may differ from a plain program's by a relative error of at most 0.0003.
Values sent between devices are 32-bit elements; how exact they have to be, the bound alone decides.
No kernel may reach another device: no remote copies, remote signals or barrier semaphores. Data moves between devices by JAX's collectives and lax.ppermute only.
A program may use at most 256 MiB of HBM per device.

v0:
```python
import math

import jax
import jax.numpy as jnp
from jax import lax
from jax.sharding import PartitionSpec as P

TA = 64
NBAND = 32
BANDW = 128
XA = 64
YA = 64


precise = lax.Precision.HIGHEST


def twiddle_table(rows_count, cols_count, modulus, direction):
    left_index = jnp.arange(rows_count, dtype=jnp.int32)[:, None]
    right_index = jnp.arange(cols_count, dtype=jnp.int32)[None, :]
    phase_angle = (left_index * right_index % modulus).astype(jnp.float32) * (
        2.0 * math.pi / modulus
    )
    return (jnp.cos(phase_angle), direction * jnp.sin(phase_angle))


def transform_last(real_part, imag_part, first_factor, second_factor, direction, real_only):
    length = first_factor * second_factor
    leading = real_part.shape[:-1]
    shaped_real = real_part.reshape(leading + (first_factor, second_factor))
    outer_real, outer_imag = twiddle_table(first_factor, first_factor, first_factor, direction)
    section_real = jnp.einsum("ka,...ab->...kb", outer_real, shaped_real, precision=precise)
    section_imag = jnp.einsum("ka,...ab->...kb", outer_imag, shaped_real, precision=precise)
    if imag_part is not None:
        shaped_imag = imag_part.reshape(leading + (first_factor, second_factor))
        section_real = section_real - jnp.einsum(
            "ka,...ab->...kb", outer_imag, shaped_imag, precision=precise
        )
        section_imag = section_imag + jnp.einsum(
            "ka,...ab->...kb", outer_real, shaped_imag, precision=precise
        )
    twist_real, twist_imag = twiddle_table(first_factor, second_factor, length, direction)
    turned_real = section_real * twist_real - section_imag * twist_imag
    turned_imag = section_real * twist_imag + section_imag * twist_real
    inner_real, inner_imag = twiddle_table(second_factor, second_factor, second_factor, direction)
    final_real = jnp.einsum("qb,...kb->...qk", inner_real, turned_real, precision=precise)
    final_real = final_real - jnp.einsum(
        "qb,...kb->...qk", inner_imag, turned_imag, precision=precise
    )
    final_real = final_real.reshape(leading + (length,))
    if real_only:
        return (final_real, None)
    final_imag = jnp.einsum("qb,...kb->...qk", inner_real, turned_imag, precision=precise)
    final_imag = final_imag + jnp.einsum(
        "qb,...kb->...qk", inner_imag, turned_real, precision=precise
    )
    return (final_real, final_imag.reshape(leading + (length,)))


def prior_gain(vertical, horizontal, total_rows, total_cols):
    fold_rows = jnp.minimum(vertical, total_rows - vertical).astype(jnp.float32) / total_rows
    fold_cols = jnp.minimum(horizontal, total_cols - horizontal).astype(jnp.float32) / total_cols
    radial_sq = fold_rows * fold_rows + fold_cols * fold_cols
    length_scale = total_rows / 64.0
    knee_sq = 1.0 / (2.0 * math.pi * length_scale) ** 2
    return 1.0 + radial_sq / 0.05 + 0.25 / jnp.sqrt(radial_sq + knee_sq)


def couple_modes(projection, kernel, band_onehot):
    kernel_freq = jnp.einsum("bmn,bf->mnf", kernel, band_onehot, precision=precise)
    return jnp.einsum("mnf,cnf->cmf", kernel_freq, projection, precision=precise)


def local(
    detector_data,
    sky_map,
    pointing,
    request_owner,
    request_block,
    beam_kernel,
    inv_white,
    mode_loading,
    mode_kernel,
):
    det_rows, samples = detector_data.shape
    rows_here, map_cols = sky_map.shape
    det_count = lax.axis_size("det")
    owners = lax.axis_size("tm")
    devices = det_count * owners
    tile_width = beam_kernel.shape[0]
    blocks_here = map_cols // tile_width
    wanted = request_owner.shape[0]
    capacity = max(2, 2 * wanted // owners)
    target = request_owner[:, 0]
    onehot_owner = (target[:, None] == jnp.arange(owners, dtype=jnp.int32)[None, :]).astype(
        jnp.int32
    )
    position = jnp.sum((jnp.cumsum(onehot_owner, axis=0) - 1) * onehot_owner, axis=1)
    slot_index = target * capacity + position
    send_ids = (
        jnp.full((owners * capacity,), blocks_here, jnp.int32).at[slot_index].set(request_block)
    )
    asked_ids = lax.all_to_all(
        send_ids.reshape(owners, capacity), "tm", split_axis=0, concat_axis=0, tiled=True
    )
    stored = sky_map.reshape(rows_here, blocks_here, tile_width).transpose(1, 0, 2)
    outgoing = jnp.take(stored, asked_ids, axis=0, mode="clip")
    arrived = lax.all_to_all(outgoing, "tm", split_axis=0, concat_axis=0, tiled=True)
    arrived_rows = arrived.reshape(owners * capacity * rows_here, tile_width)
    list_slot = pointing // rows_here
    block_row = pointing % rows_here
    row_index = (slot_index[list_slot] * rows_here + block_row).reshape(-1)
    gathered = jnp.take(arrived_rows, row_index, axis=0)
    signal = jnp.dot(gathered, beam_kernel.T, precision=precise).reshape(det_rows, samples)
    residual = detector_data - signal
    spec_real, spec_imag = transform_last(residual, None, TA, samples // TA, -1.0, False)
    frequency = jnp.arange(samples, dtype=jnp.int32)
    folded = jnp.minimum(frequency, samples - frequency)
    band_index = jnp.minimum(folded // BANDW, NBAND - 1)
    band_onehot = (jnp.arange(NBAND, dtype=jnp.int32)[:, None] == band_index[None, :]).astype(
        jnp.float32
    )
    weight_freq = jnp.dot(inv_white, band_onehot, precision=precise)
    local_proj = jnp.stack(
        [
            jnp.einsum("jm,jf->mf", mode_loading, weight_freq * spec_real, precision=precise),
            jnp.einsum("jm,jf->mf", mode_loading, weight_freq * spec_imag, precision=precise),
        ],
        axis=0,
    )
    total_proj = lax.psum(local_proj, "det")
    coupled = couple_modes(total_proj, mode_kernel, band_onehot)
    filt_real = weight_freq * (
        spec_real - jnp.einsum("jm,mf->jf", mode_loading, coupled[0], precision=precise)
    )
    filt_imag = weight_freq * (
        spec_imag - jnp.einsum("jm,mf->jf", mode_loading, coupled[1], precision=precise)
    )
    cleaned, _ = transform_last(filt_real, filt_imag, TA, samples // TA, 1.0, True)
    cleaned = cleaned / samples
    row_grads = jnp.dot(cleaned.reshape(-1, tile_width), beam_kernel, precision=precise)
    returned = jnp.zeros_like(arrived_rows).at[row_index].add(row_grads)
    returned = returned.reshape(owners, capacity, rows_here, tile_width)
    delivered = lax.all_to_all(returned, "tm", split_axis=0, concat_axis=0, tiled=True)
    accumulated = jnp.zeros((blocks_here, rows_here, tile_width), jnp.float32)
    accumulated = accumulated.at[asked_ids.reshape(-1)].add(
        delivered.reshape(-1, rows_here, tile_width), mode="drop"
    )
    data_grad = accumulated.transpose(1, 0, 2).reshape(rows_here, map_cols)
    per_device = map_cols // devices
    total_rows = rows_here * devices
    row_real, row_imag = transform_last(sky_map, None, XA, map_cols // XA, -1.0, False)
    packed = jnp.stack(
        [
            row_real.reshape(rows_here, devices, per_device),
            row_imag.reshape(rows_here, devices, per_device),
        ],
        axis=2,
    )
    packed = packed.transpose(1, 0, 2, 3).reshape(devices, rows_here, 2 * per_device)
    columns = lax.all_to_all(packed, ("det", "tm"), split_axis=0, concat_axis=0, tiled=True)
    columns = columns.reshape(total_rows, 2, per_device)
    col_real = columns[:, 0, :].T
    col_imag = columns[:, 1, :].T
    full_real, full_imag = transform_last(col_real, col_imag, YA, total_rows // YA, -1.0, False)
    device_rank = lax.axis_index("det") * owners + lax.axis_index("tm")
    col_freq = device_rank * per_device + jnp.arange(per_device, dtype=jnp.int32)
    gain_grid = prior_gain(
        jnp.arange(total_rows, dtype=jnp.int32)[None, :], col_freq[:, None], total_rows, map_cols
    )
    back_real, back_imag = transform_last(
        full_real * gain_grid, full_imag * gain_grid, YA, total_rows // YA, 1.0, False
    )
    stacked = jnp.stack([back_real, back_imag], axis=0).reshape(2, per_device, devices, rows_here)
    stacked = stacked.transpose(2, 3, 0, 1).reshape(devices, rows_here, 2 * per_device)
    returned_rows = lax.all_to_all(stacked, ("det", "tm"), split_axis=0, concat_axis=0, tiled=True)
    returned_rows = returned_rows.reshape(devices, rows_here, 2, per_device)
    spec_rows_real = returned_rows[:, :, 0, :].transpose(1, 0, 2).reshape(rows_here, map_cols)
    spec_rows_imag = returned_rows[:, :, 1, :].transpose(1, 0, 2).reshape(rows_here, map_cols)
    prior_term, _ = transform_last(spec_rows_real, spec_rows_imag, XA, map_cols // XA, 1.0, True)
    prior_term = prior_term / (total_rows * map_cols)
    return data_grad - prior_term


def solution(mesh):
    return jax.shard_map(
        local,
        mesh=mesh,
        in_specs=(
            P("det", "tm"),
            P(("det", "tm"), None),
            P("det", "tm"),
            P(("det", "tm"), None),
            P(("det", "tm")),
            P(),
            P("det", None),
            P("det", None),
            P(),
        ),
        out_specs=P(("det", "tm"), None),
        check_vma=False,
    )
```

profile of v0, /device:TPU:0, one launch (start us, length us, event | category | flops | bytes accessed | tf_op | source)
XLA Modules:
  0.0 611.3 jit_solution(10162685909855062625)
XLA Ops:
  10.3 8.0 %all-to-all-start = ((s32[16,1,2]{2,1,0:T(1,128)}), s32[16,1,2]{2,1,0:T(1,128)S(1)}, u32[]{:S(2)}, u32[]{:S(2)}) async-start(s32[16,1,2]{2,1,0:T(1,128)} %bitcast.3), calls=%async_computation | async-start | bytes 16384 | tf_op jit(solution)/shard_map/all_to_all | solution.py:103
  19.8 24.7 %gather_fusion = s32[4096]{0:T(1024)S(1)} fusion(s32[16]{0:T(128)S(1)} %multiply_add_fusion.3, s32[4096]{0:T(1024)S(1)} %broadcast_clamp_fusion.1), kind=kCustom, calls=%fused_computation | custom fusion | bytes 49152 | tf_op jit(solution)/shard_map/gather | solution.py:112
  52.3 5.6 fusion.54
  57.8 32.3 %copy.95 = f32[16,16,8192]{1,0,2:T(8,128)} copy(f32[16,16,8192]{2,1,0:T(8,128)} %bitcast.349) | data formatting | bytes 16777216 | tf_op jit(solution)/shard_map/bmn,bf->mnf/dot_general | solution.py:70
  98.0 7.4 %all-to-all-start.1 = ((f32[16,2,32,128]{3,2,1,0:T(8,128)}), f32[16,2,32,128]{3,2,1,0:T(8,128)S(1)}, u32[]{:S(2)}, u32[]{:S(2)}) async-start(f32[16,2,32,128]{3,2,1,0:T(8,128)} %bitcast.8), calls=%async_computation.1 | async-start | bytes 1048576 | tf_op jit(solution)/shard_map/all_to_all | solution.py:108
  107.8 8.6 %all-to-all-done.1 = f32[16,2,32,128]{3,2,1,0:T(8,128)S(1)} async-done(((f32[16,2,32,128]{3,2,1,0:T(8,128)}), f32[16,2,32,128]{3,2,1,0:T(8,128)S(1)}, u32[]{:S(2)}, u32[]{:S(2)}) %all-to-all-start.1) | async-done | bytes 524320 | tf_op jit(solution)/shard_map/all_to_all | solution.py:108
  116.4 6.9 %all-to-all-start.3 = ((f32[128,32,128]{2,1,0:T(8,128)}), f32[128,32,128]{2,1,0:T(8,128)}, u32[]{:S(2)}, u32[]{:S(2)}) async-start(f32[128,32,128]{2,1,0:T(8,128)} %copy.99), calls=%async_computation.3 | async-start | bytes 4194304 | tf_op jit(solution)/shard_map/all_to_all | solution.py:161
  123.3 10.8 %gather_fusion.2 = f32[4096,128]{1,0:T(8,128)S(1)} fusion(f32[1024,128]{1,0:T(8,128)S(1)} %bitcast.348, s32[4096]{0:T(1024)S(1)} %broadcast_clamp_fusion), kind=kCustom, calls=%fused_computation.2 | custom fusion | bytes 4210688 | tf_op jit(solution)/shard_map/jit(_take)/gather | solution.py:113
  134.1 5.7 fusion.24
  161.1 5.2 reshape.318
  166.3 5.6 subtract_bitcast_fusion.1
  175.7 4.9 reshape.317
  186.8 63.2 %all-reduce.2.cloned.1.call-done = f32[2,16,8192]{2,1,0:T(8,128)} async-done(((f32[2,16,8192]{2,1,0:T(8,128)}), f32[2,16,8192]{2,1,0:T(8,128)}) %all-reduce.2.cloned.1.call-update) | async-done | bytes 1048592 | tf_op jit(solution)/shard_map/psum | solution.py:131
  250.0 9.9 %copy.94 = f32[2,16,8192]{1,0,2:T(2,128)} copy(f32[2,16,8192]{2,1,0:T(8,128)} %all-reduce.2.cloned.1.call-done) | data formatting | bytes 2097152 | tf_op jit(solution)/shard_map/psum | solution.py:131
  259.9 109.6 %convolution_bitcast_fusion.5 = f32[2,16,8192]{1,0,2:T(2,128)S(1)} fusion(f32[2,16,8192]{1,0,2:T(2,128)} %copy.94, f32[16,16,8192]{1,0,2:T(8,128)} %copy.95), kind=kOutput, calls=%fused_computation.15 | convolution fusion | flops 50331648 | bytes 10485760 | tf_op jit(solution)/shard_map/mnf,cnf->cmf/dot_general | solution.py:71
  369.5 7.0 %fusion.414 = (f32[1,16,8192]{1,0,2:T(1,128)S(1)}, f32[1,16,8192]{1,0,2:T(1,128)S(1)}) fusion(f32[2,16,8192]{1,0,2:T(2,128)S(1)} %convolution_bitcast_fusion.5), kind=kLoop, calls=%fused_computation.457 | loop fusion | bytes 2097152 | tf_op jit(solution)/shard_map/slice | solution.py:137
  376.6 5.0 fusion.29
  381.5 5.0 fusion.28
  409.6 23.8 %scatter_custom_fusion.1 = f32[1024,128]{1,0:T(8,128)} fusion(s32[4096]{0:T(1024)S(1)} %bitcast.371, f32[4096,128]{1,0:T(8,128)} %fusion.416, f32[]{:T(128)} %constant.180.clone.1), kind=kCustom, calls=%fused_computation.121 | custom fusion | flops 524288 | bytes 524800 | tf_op jit(solution)/shard_map/scatter-add | solution.py:142
  433.4 6.9 %all-to-all-start.2 = ((f32[16,2,32,128]{3,2,1,0:T(8,128)}), f32[16,2,32,128]{3,2,1,0:T(8,128)S(1)}, u32[]{:S(2)}, u32[]{:S(2)}) async-start(f32[16,2,32,128]{3,2,1,0:T(8,128)} %bitcast.35), calls=%async_computation.2 | async-start | bytes 1048576 | tf_op jit(solution)/shard_map/all_to_all | solution.py:144
  440.3 5.6 reshape.325
  446.0 8.1 %fusion.415 = (f32[4096,1,64]{2,1,0:T(1,128)}, f32[4096,1,64]{2,1,0:T(1,128)}) fusion(f32[4096,2,64]{2,1,0:T(2,128)} %reshape.325), kind=kLoop, calls=%fused_computation.458 | loop fusion | bytes 4194304 | tf_op jit(solution)/shard_map/slice | solution.py:164
  457.2 4.8 fusion.148
  462.0 4.8 fusion.130
  470.1 5.3 convolution_subtract_fusion.1
  486.5 4.4 fusion.9
  494.9 4.8 fusion.8
  507.3 5.1 fusion.68
  512.5 5.0 subtract_bitcast_fusion
  521.6 7.1 %add_bitcast_fusion = f32[64,64,64]{1,2,0:T(8,128)} fusion(f32[64,64,64]{2,1,0:T(8,128)} %fusion.68, f32[64,64,64]{2,1,0:T(8,128)} %copy-done.3, f32[64,64,64]{2,1,0:T(8,128)S(1)} %convolution_subtract_fusion, f32[64,64]{0,1:T(8,128)S(1)} %copy.113, f32[64,64]{0,1:T(8,128)S(1)} %copy.104), kind=kOutput, calls=%fused_computation.52 | convolution fusion | flops 202432512 | bytes 4227072 | tf_op jit(solution)/shard_map/qb,...kb->...qk/dot_general | solution.py:54
  543.5 8.0 %all-to-all-start.4 = ((f32[128,32,128]{2,1,0:T(8,128)}), f32[128,32,128]{2,1,0:T(8,128)S(1)}, u32[]{:S(2)}, u32[]{:S(2)}) async-start(f32[128,32,128]{2,1,0:T(8,128)} %copy.121), calls=%async_computation.4 | async-start | bytes 4194304 | tf_op jit(solution)/shard_map/all_to_all | solution.py:176
  556.4 24.8 %all-to-all-done.4 = f32[128,32,128]{2,1,0:T(8,128)S(1)} async-done(((f32[128,32,128]{2,1,0:T(8,128)}), f32[128,32,128]{2,1,0:T(8,128)S(1)}, u32[]{:S(2)}, u32[]{:S(2)}) %all-to-all-start.4) | async-done | bytes 2097184 | tf_op jit(solution)/shard_map/all_to_all | solution.py:176
  (150 shorter events, 152.9 us)
Async XLA Ops:
  6.5 45.7 %copy-start = (f32[32,16,16]{0,2,1:T(8,128)S(1)}, f32[32,16,16]{0,2,1:T(8,128)}, u32[]{:S(2)}) copy-start(f32[32,16,16]{0,2,1:T(8,128)} %param.17) | copy-start | bytes 98308
  10.3 86.2 %all-to-all-start = ((s32[16,1,2]{2,1,0:T(1,128)}), s32[16,1,2]{2,1,0:T(1,128)S(1)}, u32[]{:S(2)}, u32[]{:S(2)}) async-start(s32[16,1,2]{2,1,0:T(1,128)} %bitcast.3), calls=%async_computation | async-start | bytes 16384 | tf_op jit(solution)/shard_map/all_to_all | solution.py:103
  19.8 24.8 %copy-start.17 = (s32[64,64]{1,0:T(8,128)S(1)}, s32[64,64]{1,0:T(8,128)}, u32[]{:S(2)}) copy-start(s32[64,64]{1,0:T(8,128)} %param.11) | copy-start | bytes 49156
  19.8 25.2 %copy-start.13 = (f32[32,8192]{1,0:T(8,128)S(1)}, f32[32,8192]{1,0:T(8,128)}, u32[]{:S(2)}) copy-start(f32[32,8192]{1,0:T(8,128)} %param.10) | copy-start | bytes 3145732
  94.4 2.2 copy-start.14
  96.4 9.0 %copy-start.19 = (f32[64,32]{0,1:T(8,128)S(1)}, f32[64,32]{0,1:T(8,128)}, u32[]{:S(2)}) copy-start(f32[64,32]{0,1:T(8,128)} %param.15) | copy-start | bytes 24580
  98.0 18.4 %all-to-all-start.1 = ((f32[16,2,32,128]{3,2,1,0:T(8,128)}), f32[16,2,32,128]{3,2,1,0:T(8,128)S(1)}, u32[]{:S(2)}, u32[]{:S(2)}) async-start(f32[16,2,32,128]{3,2,1,0:T(8,128)} %bitcast.8), calls=%async_computation.1 | async-start | bytes 1048576 | tf_op jit(solution)/shard_map/all_to_all | solution.py:108
  116.4 317.0 %all-to-all-start.3 = ((f32[128,32,128]{2,1,0:T(8,128)}), f32[128,32,128]{2,1,0:T(8,128)}, u32[]{:S(2)}, u32[]{:S(2)}) async-start(f32[128,32,128]{2,1,0:T(8,128)} %copy.99), calls=%async_computation.3 | async-start | bytes 4194304 | tf_op jit(solution)/shard_map/all_to_all | solution.py:161
  123.2 126.8 %all-reduce.2.cloned.1.call-start = ((), (), s32[]{:S(2)}) async-start(), calls=%async_computation.5 | async-start | bytes 2097152 | tf_op jit(solution)/shard_map/psum | solution.py:131
  123.3 10.8 %copy-start.16 = (f32[128,128]{1,0:T(8,128)S(1)}, f32[128,128]{1,0:T(8,128)}, u32[]{:S(2)}) copy-start(f32[128,128]{1,0:T(8,128)} %param.14) | copy-start | bytes 196612
  148.1 5.6 copy-start.2
  175.7 4.9 copy-start.4
  175.7 4.9 copy-start.18
  180.7 3.0 copy-start.6
  369.5 7.0 %copy-start.5 = (f32[64,8192]{1,0:T(8,128)S(1)}, f32[64,8192]{1,0:T(8,128)}, u32[]{:S(2)}) copy-start(f32[64,8192]{1,0:T(8,128)} %reshape.318) | copy-start | bytes 6291460
  376.5 5.0 copy-start.7
  433.4 109.4 %all-to-all-start.2 = ((f32[16,2,32,128]{3,2,1,0:T(8,128)}), f32[16,2,32,128]{3,2,1,0:T(8,128)S(1)}, u32[]{:S(2)}, u32[]{:S(2)}) async-start(f32[16,2,32,128]{3,2,1,0:T(8,128)} %bitcast.35), calls=%async_computation.2 | async-start | bytes 1048576 | tf_op jit(solution)/shard_map/all_to_all | solution.py:144
  470.1 5.3 copy-start.8
  503.6 8.8 %copy-start.3 = (f32[64,64,64]{2,1,0:T(8,128)}, f32[64,64,64]{2,1,0:T(8,128)S(1)}, u32[]{:S(2)}) copy-start(f32[64,64,64]{2,1,0:T(8,128)S(1)} %convolution_add_fusion) | copy-start | bytes 3145732
  528.7 4.3 copy-start.9
  542.8 0.8 copy-start.15
  543.5 37.7 %all-to-all-start.4 = ((f32[128,32,128]{2,1,0:T(8,128)}), f32[128,32,128]{2,1,0:T(8,128)S(1)}, u32[]{:S(2)}, u32[]{:S(2)}) async-start(f32[128,32,128]{2,1,0:T(8,128)} %copy.121), calls=%async_computation.4 | async-start | bytes 4194304 | tf_op jit(solution)/shard_map/all_to_all | solution.py:176
  556.4 26.8 %copy-start.10 = (f32[64,32,128]{2,1,0:T(8,128)}, f32[64,32,128]{2,1,0:T(8,128)S(1)}, u32[]{:S(2)}) copy-start(f32[64,32,128]{2,1,0:T(8,128)S(1)} %scatter_fusion) | copy-start | bytes 3145732
  593.4 2.5 copy-start.12
  600.2 1.6 copy-start.11
  600.2 3.9 copy-start.1
Sparse Core Ops, SparseCore 0:
  186.2 63.7 all-reduce.1
where the time goes:
time: 623 us; the launch traced here: 611 us
  matrix products  257 us (41%)
  local copies, waits for them, and re-layouts  164 us (26%)
  waiting for transfers between devices  96.7 us (16%)
  other arithmetic  42 us (7%)
  starting transfers between devices  37.2 us (6%)
  between operations  14.5 us (2%)
    dot_general x1, matrix products, couple_modes(): jnp.einsum('mnf,cnf->cmf', kernel_freq, projection, precision=precise)  110 us
    psum x1, waiting for transfers between devices, local(): total_proj = lax.psum(local_proj, 'det')  63.2 us
    dot_general x1, local copies, waits for them, and re-layouts, couple_modes(): jnp.einsum('bmn,bf->mnf', kernel, band_onehot, precision=precise)  32.3 us
    all_to_all x1, waiting for transfers between devices, local(): lax.all_to_all(stacked, ('det', 'tm'), split_axis=0, concat_axis=0, tiled...  24.8 us
    gather x1, local copies, waits for them, and re-layouts, local(): row_index = (slot_index[list_slot] * rows_here + block_row).reshape(-1)  24.7 us
    scatter-add x1, other arithmetic, local(): returned = jnp.zeros_like(arrived_rows).at[row_index].add(row_grads)  23.8 us
    dot_general x6, matrix products, transform_last(): jnp.einsum('qb,...kb->...qk', inner_imag, turned_imag, precision=precise)  20.8 us
    dot_general x4, matrix products, transform_last(): jnp.einsum('qb,...kb->...qk', inner_imag, turned_real, precision=precise)  16.7 us
  transfers between devices with their start and end apart: 6, of which 3 were waited for; matrix products, arithmetic and copies ran while one was open for 71% of the time, Pallas kernels for 0%

commit v1 on v0

v1 whole, which is shorter than its diff:
```python
import math

import jax
import jax.numpy as jnp
import numpy as np
from jax import lax
from jax.experimental import pallas as pl
from jax.experimental.pallas import tpu as pltpu
from jax.sharding import PartitionSpec as P

NBAND = 32
F32 = jnp.float32
BF16 = jnp.bfloat16
VM = pltpu.VMEM


def halves(table):
    high = np.asarray(table, np.float32).astype(BF16)
    low = (np.asarray(table, np.float64) - high.astype(np.float64)).astype(BF16)
    return high, low


def wave(rows, cols, period):
    turn = 2.0 * math.pi * ((rows[:, None] * cols[None, :]) % period) / period
    return np.cos(turn), np.sin(turn)


def stage_tables(width, copies):
    index = np.arange(width, dtype=np.float64)
    cos, sin = wave(index, index, width)
    half_cos, half_sin = wave(index, index + 0.5, width)
    eye = np.eye(copies)
    cos, sin = np.kron(eye, cos), np.kron(eye, sin)
    cas_half = np.kron(eye, half_cos + half_sin)
    zero = np.zeros_like(cos)
    general = np.block([[cos, -sin], [sin, cos]])
    special = np.block([[cos + sin, zero], [zero, cas_half]])
    return general, special


def row_tables():
    general, special = stage_tables(128, 1)
    return general, special


def twiddles(first, second, length):
    return [
        np.asarray(t, np.float32)
        for t in wave(np.arange(first, dtype=np.float64), second.astype(np.float64), length)
    ]


def real_left_table():
    index = np.arange(64, dtype=np.float64)
    cos, sin = wave(index, np.arange(128, dtype=np.float64), 128)
    forward = np.concatenate([cos, -sin], axis=0)
    forward[64] = np.cos(math.pi * np.arange(128))
    inverse = 2.0 * forward.T
    inverse[:, 0] = 1.0
    inverse[:, 64] = forward[64]
    return forward, inverse


def band_tables():
    second = np.arange(128)
    general = np.minimum(np.minimum(second, 127 - second) // 2, NBAND - 1)
    special = np.minimum(np.minimum(second, 128 - second) // 2, NBAND - 1)
    bands = np.arange(NBAND)[:, None]
    return (bands == general[None]).astype(np.float32), (bands == special[None]).astype(np.float32)


def turn_by(pair, quotient, count, sign):
    real, imag = pair
    cos = math.cos(2.0 * math.pi * quotient / count)
    sin = sign * math.sin(2.0 * math.pi * quotient / count)
    if 8 * quotient == count:
        scale = math.sqrt(0.5)
        if sign < 0:
            return (real + imag) * scale, (imag - real) * scale
        return (real - imag) * scale, (imag + real) * scale
    return real * cos - imag * sin, real * sin + imag * cos


def real_transform(values):
    count = len(values)
    if count == 1:
        return [(values[0], None)]
    if count == 2:
        return [(values[0] + values[1], None), (values[0] - values[1], None)]
    even = real_transform(values[0::2])
    odd = real_transform(values[1::2])
    half = count // 2
    out = [None] * (half + 1)
    out[0] = (even[0][0] + odd[0][0], None)
    out[half] = (even[0][0] - odd[0][0], None)
    for k in range(1, half // 2):
        turned = turn_by(odd[k], k, count, -1.0)
        out[k] = (even[k][0] + turned[0], even[k][1] + turned[1])
        out[half - k] = (even[k][0] - turned[0], turned[1] - even[k][1])
    out[half // 2] = (even[half // 2][0], -odd[half // 2][0])
    return out


def real_inverse(spectrum, count):
    if count == 1:
        return [spectrum[0][0]]
    first, last = spectrum[0][0], spectrum[count // 2][0]
    if count == 2:
        return [first + last, first - last]
    half = count // 2
    even = [None] * (half // 2 + 1)
    odd = [None] * (half // 2 + 1)
    even[0] = (first + last, None)
    odd[0] = (first - last, None)
    for k in range(1, half // 2):
        one, two = spectrum[k], spectrum[half - k]
        even[k] = (one[0] + two[0], one[1] - two[1])
        odd[k] = turn_by((one[0] - two[0], one[1] + two[1]), k, count, 1.0)
    middle = spectrum[half // 2]
    even[half // 2] = (middle[0] + middle[0], None)
    odd[half // 2] = (-(middle[1] + middle[1]), None)
    out = [None] * count
    out[0::2] = real_inverse(even, half)
    out[1::2] = real_inverse(odd, half)
    return out


def forward_tile(values, cos_ref, sin_ref, store):
    spectrum = real_transform(values)
    store(0, spectrum[0][0], spectrum[32][0])
    for k in range(1, 32):
        real, imag = spectrum[k]
        cos, sin = cos_ref[k : k + 1, :], sin_ref[k : k + 1, :]
        store(k, real * cos + imag * sin, imag * cos - real * sin)


def inverse_tile(load, cos_ref, sin_ref):
    first, last = load(0)
    spectrum = [(first, None)]
    for k in range(1, 32):
        real, imag = load(k)
        cos, sin = cos_ref[k : k + 1, :], sin_ref[k : k + 1, :]
        spectrum.append((real * cos - imag * sin, imag * cos + real * sin))
    spectrum.append((last, None))
    return real_inverse(spectrum, 64)


def parts(value):
    high = value.astype(BF16)
    return high, (value - high.astype(F32)).astype(BF16)


def mm(left, right):
    return jnp.dot(left, right, preferred_element_type=F32)


def mm_right(value, high, low):
    top, rest = parts(value)
    return mm(top, high) + mm(rest, high) + mm(top, low)


def mm_left(high, low, value):
    top, rest = parts(value)
    return mm(high, top) + mm(high, rest) + mm(low, top)


def mm_both(left, right):
    high, low = parts(right)
    return mm_right(left, high, low)


def aligned(index, size):
    return pl.ds(pl.multiple_of(index * size, size), size)


def ids_kernel(owner, block, send, slots, counts):
    for i in range(16):
        counts[i] = 0
    row = lax.broadcasted_iota(jnp.int32, (16, 128), 0)
    lane = lax.broadcasted_iota(jnp.int32, (16, 128), 1)
    table = jnp.full((16, 128), 64, jnp.int32)
    for i in range(16):
        target = owner[i]
        place = counts[target]
        counts[target] = place + 1
        slots[i] = target * 2 + place
        table = jnp.where((row == target) & (lane == place), block[i], table)
    send[...] = table


def pick_kernel(asked, sky, out):
    def step(i, carry):
        for c in range(2):
            block = jnp.minimum(asked[i, c], 63)
            out[2 * i + c] = sky[:, aligned(block, 128)]
        return carry

    lax.fori_loop(0, 16, step, 0)


def prep_kernel(inv_white, band, band_zero, kernel, weight, weight_zero, couple, couple_zero):
    for source, onehot, out in (
        (inv_white, band, weight),
        (inv_white, band_zero, weight_zero),
        (kernel, band, couple),
        (kernel, band_zero, couple_zero),
    ):
        out[...] = jnp.dot(
            source[...], onehot[...], precision=lax.Precision.HIGHEST, preferred_element_type=F32
        )


def rows_kernel(sky, cos, sin, gen_h, gen_l, spe_h, spe_l, out, work, done):
    def tile(i, carry):
        rows = aligned(i, 8)
        values = [sky[rows, 128 * u : 128 * u + 128] for u in range(64)]

        def store(k, real, imag):
            work[k, rows, 0:128] = real
            work[k, rows, 128:256] = imag

        forward_tile(values, cos, sin, store)
        return carry

    lax.fori_loop(0, 4, tile, 0)
    for q in range(2):
        chunk = work[16 * q : 16 * q + 16].reshape(512, 256)
        done[512 * q : 512 * q + 512] = mm_right(chunk, gen_h[...], gen_l[...])
    done[0:32] = mm_right(work[0], spe_h[...], spe_l[...])
    for t in range(8):
        for c in range(2):
            block = done[128 * t : 128 * t + 128, 128 * c : 128 * c + 128]
            out[:, 1024 * c + 128 * t : 1024 * c + 128 * t + 128] = block.T


def columns_kernel(
    rank, data, left_h, left_l, cos, sin, gen_h, gen_l, spe_h, spe_l, gent_h, gent_l, spet_h, spet_l,
    back_h, back_l, out, work, gained,
):
    for q in range(4):
        lanes = slice(512 * q, 512 * q + 512)
        both = mm_left(left_h[...], left_l[...], data[:, lanes])
        for s in range(4):
            t = 4 * q + s
            real, imag = both[0:64, 128 * s : 128 * s + 128], both[64:128, 128 * s : 128 * s + 128]
            work[t, :, 0:128] = real * cos[...] + imag * sin[...]
            work[t, :, 128:256] = imag * cos[...] - real * sin[...]
    total_rows, total_cols = 4096, 8192
    row = lax.broadcasted_iota(jnp.int32, (64, 128), 0)
    lane = lax.broadcasted_iota(jnp.int32, (64, 128), 1)
    squares = []
    for part in range(2):
        vertical = row + 128 * (lane % 32)
        if part:
            vertical = jnp.where(row == 0, 64 + 128 * (lane % 32), vertical)
        folded = jnp.minimum(vertical, total_rows - vertical).astype(F32) / total_rows
        squares.append(folded * folded)
    lane8 = lax.broadcasted_iota(jnp.int32, (8, 128), 1)
    base = rank[0] * 64
    knee_sq = 1.0 / (2.0 * math.pi * (total_rows / 64.0)) ** 2
    special = lax.broadcasted_iota(jnp.int32, (16, 8, 256), 1) == 0
    for q in range(2):
        tiles = slice(8 * q, 8 * q + 8)
        gained[tiles] = mm_right(
            work[tiles].reshape(512, 256), gen_h[...], gen_l[...]
        ).reshape(8, 64, 256)
    zero = mm_right(work[:, 0:8, :].reshape(128, 256), spe_h[...], spe_l[...]).reshape(16, 8, 256)
    gained[:, 0:8, :] = jnp.where(special, zero, gained[:, 0:8, :])

    def gain_tile(t, carry):
        first = 4 * (t % 8) + lane8 // 32
        first = jnp.where((first == 0) & (t == 8), 32, first)
        horizontal = base + first
        folded = jnp.minimum(horizontal, total_cols - horizontal).astype(F32) / total_cols
        across = (folded * folded)[0:1]
        for part in range(2):
            radial = squares[part] + across
            gain = 1.0 + radial * (1.0 / 0.05) + 0.25 * lax.rsqrt(radial + knee_sq)
            lanes = slice(128 * part, 128 * part + 128)
            gained[t, :, lanes] = gained[t, :, lanes] * (-gain)
        return carry

    lax.fori_loop(0, 16, gain_tile, 0)
    for q in range(2):
        tiles = slice(8 * q, 8 * q + 8)
        work[tiles] = mm_right(
            gained[tiles].reshape(512, 256), gent_h[...], gent_l[...]
        ).reshape(8, 64, 256)
    zero = mm_right(gained[:, 0:8, :].reshape(128, 256), spet_h[...], spet_l[...])
    work[:, 0:8, :] = jnp.where(special, zero.reshape(16, 8, 256), work[:, 0:8, :])
    for q in range(4):
        pieces = []
        for s in range(4):
            real, imag = work[4 * q + s, :, 0:128], work[4 * q + s, :, 128:256]
            pieces.append(
                jnp.concatenate(
                    [real * cos[...] - imag * sin[...], imag * cos[...] + real * sin[...]], axis=0
                )
            )
        both = jnp.concatenate(pieces, axis=1)
        out[:, 512 * q : 512 * q + 512] = mm_left(back_h[...], back_l[...], both)


def rows_back_kernel(data, cos, sin, gent_h, gent_l, spet_h, spet_l, out, work, done):
    for t in range(8):
        for c in range(2):
            block = data[:, 1024 * c + 128 * t : 1024 * c + 128 * t + 128]
            work[128 * t : 128 * t + 128, 128 * c : 128 * c + 128] = block.T
    for q in range(2):
        chunk = work[512 * q : 512 * q + 512]
        done[16 * q : 16 * q + 16] = mm_right(chunk, gent_h[...], gent_l[...]).reshape(16, 32, 256)
    done[0] = mm_right(work[0:32], spet_h[...], spet_l[...])

    def tile(i, carry):
        rows = aligned(i, 8)

        def load(k):
            return done[k, rows, 0:128], done[k, rows, 128:256]

        values = inverse_tile(load, cos, sin)
        for u in range(64):
            out[rows, 128 * u : 128 * u + 128] = values[u]
        return carry

    lax.fori_loop(0, 4, tile, 0)


def detect_kernel(
    slots, pointing, data, arrived, beam_t, cos, sin, gen_h, gen_l, spe_h, spe_l, weight, weight_zero,
    loading, spectrum, projected, points, picked, table, onehot, signal, work,
):
    for i in range(16):
        picked[32 * i : 32 * i + 32] = arrived[slots[i]]
    high, low = parts(mm_both(picked[...], beam_t[...]))
    table[:, 0:128] = high
    table[:, 128:256] = low
    points[:, 0:64] = pointing[...]
    points[:, 64:128] = pointing[...]
    lane = lax.broadcasted_iota(jnp.int32, (64, 512), 1)

    def gather(c, carry):
        turned = pltpu.roll(points[...], (128 - 8 * c) % 128, 1)
        for u in range(8):
            hit = turned[:, u : u + 1] == lane
            onehot[64 * u : 64 * u + 64] = jnp.where(hit, 1.0, 0.0).astype(BF16)
        both = mm(onehot[...], table[...])
        signal[aligned(c, 8)] = (both[:, 0:128] + both[:, 128:256]).reshape(8, 64, 128)
        return carry

    lax.fori_loop(0, 8, gather, 0)

    def tile(i, carry):
        rows = aligned(i, 8)
        values = [data[rows, 128 * u : 128 * u + 128] - signal[u, rows, :] for u in range(64)]

        def store(k, real, imag):
            work[k, rows, 0:128] = real
            work[k, rows, 128:256] = imag

        forward_tile(values, cos, sin, store)
        return carry

    lax.fori_loop(0, 8, tile, 0)

    def stage(q, carry):
        chunk = work[aligned(q, 8)].reshape(512, 256)
        spectrum[aligned(q, 8)] = mm_right(chunk, gen_h[...], gen_l[...]).reshape(8, 64, 256)
        return carry

    lax.fori_loop(0, 4, stage, 0)
    spectrum[0] = mm_right(work[0], spe_h[...], spe_l[...])
    left_h, left_l = parts(loading[...].T)

    def project(k, carry):
        first = jnp.where(k == 0, weight_zero[...], weight[...])
        scale = jnp.concatenate([first, weight[...]], axis=1)
        projected[k] = mm_left(left_h, left_l, spectrum[k] * scale)
        return carry

    lax.fori_loop(0, 32, project, 0)


def couple_kernel(place, shares, couple, couple_zero, out):
    def one(k, carry):
        total = shares[0, k]
        for s in range(1, shares.shape[0]):
            total = total + shares[s, k]
        pick = (place[0] == 0) & (k == 0)
        real = jnp.zeros((16, 128), F32)
        imag = jnp.zeros((16, 128), F32)
        for n in range(16):
            factor = couple[16 * n : 16 * n + 16]
            first = jnp.where(pick, couple_zero[16 * n : 16 * n + 16], factor)
            real = real + first * total[n : n + 1, 0:128]
            imag = imag + factor * total[n : n + 1, 128:256]
        out[k, :, 0:128] = real
        out[k, :, 128:256] = imag
        return carry

    lax.fori_loop(0, 4, one, 0)


def clean_kernel(
    slots, points, coupled, spectrum, weight, weight_zero, loading, beam, cos, sin, gent_h, gent_l,
    spet_h, spet_l, out, filtered, work, cleaned, onehot, total,
):
    left_h, left_l = parts(loading[...])

    def remove(k, carry):
        first = jnp.where(k == 0, weight_zero[...], weight[...])
        scale = jnp.concatenate([first, weight[...]], axis=1)
        filtered[k] = scale * (spectrum[k] - mm_left(left_h, left_l, coupled[k]))
        return carry

    lax.fori_loop(0, 32, remove, 0)

    def stage(q, carry):
        chunk = filtered[aligned(q, 8)].reshape(512, 256)
        work[aligned(q, 8)] = mm_right(chunk, gent_h[...], gent_l[...]).reshape(8, 64, 256)
        return carry

    lax.fori_loop(0, 4, stage, 0)
    work[0] = mm_right(filtered[0], spet_h[...], spet_l[...])

    def tile(i, carry):
        rows = aligned(i, 8)

        def load(k):
            return work[k, rows, 0:128], work[k, rows, 128:256]

        values = inverse_tile(load, cos, sin)
        for u in range(64):
            cleaned[u, rows, :] = values[u]
        return carry

    lax.fori_loop(0, 8, tile, 0)
    sub = lax.broadcasted_iota(jnp.int32, (512, 512), 0)
    total[...] = jnp.zeros((512, 256), F32)

    def scatter(c, carry):
        hit = points[pl.ds(c, 1), :] == sub
        onehot[...] = jnp.where(hit, 1.0, 0.0).astype(BF16)
        high, low = parts(cleaned[aligned(c, 8)].reshape(512, 128))
        total[...] += mm(onehot[...], jnp.concatenate([high, low], axis=1))
        return carry

    lax.fori_loop(0, 8, scatter, 0)
    summed = total[:, 0:128] + total[:, 128:256]
    grads = mm_both(summed, beam[...])
    out[...] = jnp.zeros((32, 32, 128), F32)
    for i in range(16):
        out[slots[i]] = grads[32 * i : 32 * i + 32]


def final_kernel(asked, delivered, prior, out):
    out[...] = prior[...]

    def step(i, carry):
        for c in range(2):
            block = asked[i, c]

            @pl.when(block < 64)
            def _():
                lanes = aligned(block, 128)
                out[:, lanes] = out[:, lanes] + delivered[2 * i + c]

        return carry

    lax.fori_loop(0, 16, step, 0)


SM = pltpu.SMEM


def call(kernel, ins, outs, scratch=(), out_spaces=None, spaces=None):
    spaces = spaces or {}
    in_specs = [pl.BlockSpec(memory_space=spaces.get(i, VM)) for i in range(len(ins))]
    out_spaces = out_spaces or [VM] * len(outs)
    out_specs = [pl.BlockSpec(memory_space=s) for s in out_spaces]
    shapes = [jax.ShapeDtypeStruct(s, d) for s, d in outs]
    result = pl.pallas_call(
        kernel,
        out_shape=shapes,
        in_specs=in_specs,
        out_specs=out_specs,
        scratch_shapes=list(scratch),
        compiler_params=pltpu.CompilerParams(vmem_limit_bytes=48 * 1024 * 1024),
        name=kernel.__name__,
    )(*ins)
    return result if len(outs) > 1 else result[0]


def row_constants():
    general, special = row_tables()
    cos, sin = twiddles(32, np.arange(128), 8192)
    scale = 2.0**-13
    return (
        (cos, sin),
        (*halves(general), *halves(special)),
        (*halves(general.T * scale), *halves(special.T * scale)),
    )


def col_constants():
    general, special = stage_tables(32, 4)
    left, back = real_left_table()
    cos, sin = twiddles(64, np.arange(128) % 32, 4096)
    return (
        (*halves(left), cos, sin),
        (*halves(general), *halves(special), *halves(general.T), *halves(special.T)),
        halves(back * 2.0**-12),
    )


def local(
    detector_data,
    sky_map,
    pointing,
    request_owner,
    request_block,
    beam_kernel,
    inv_white,
    mode_loading,
    mode_kernel,
):
    turn, ahead, behind = row_constants()
    start, middle, end = col_constants()
    band, band_zero = band_tables()
    det_rank = lax.axis_index("det")
    rank = (det_rank * lax.axis_size("tm") + lax.axis_index("tm")).astype(jnp.int32).reshape(1)

    send, slots = call(
        ids_kernel,
        (request_owner.reshape(16), request_block),
        [((16, 128), jnp.int32), ((16,), jnp.int32)],
        [SM((16,), jnp.int32)],
        [VM, SM],
        {0: SM, 1: SM},
    )
    asked = lax.all_to_all(send, "tm", split_axis=0, concat_axis=0, tiled=True)
    outgoing = call(pick_kernel, (asked, sky_map), [((32, 32, 128), F32)], spaces={0: SM})
    arrived = lax.all_to_all(outgoing, "tm", split_axis=0, concat_axis=0, tiled=True)

    packed = call(
        rows_kernel,
        (sky_map, *turn, *ahead),
        [((128, 2048), F32)],
        [VM((32, 32, 256), F32), VM((1024, 256), F32)],
    )
    columns = lax.all_to_all(packed, ("det", "tm"), split_axis=0, concat_axis=0, tiled=True)

    weight, weight_zero, couple, couple_zero = call(
        prep_kernel,
        (inv_white, band, band_zero, mode_kernel.transpose(2, 1, 0).reshape(256, NBAND)),
        [((64, 128), F32), ((64, 128), F32), ((256, 128), F32), ((256, 128), F32)],
    )
    spectrum, projected = call(
        detect_kernel,
        (
            slots, pointing, detector_data, arrived, beam_kernel.T, *turn, *ahead, weight, weight_zero,
            mode_loading,
        ),
        [((32, 64, 256), F32), ((32, 16, 256), F32)],
        [
            VM((64, 128), jnp.int32),
            VM((512, 128), F32),
            VM((512, 256), BF16),
            VM((512, 512), BF16),
            VM((64, 64, 128), F32),
            VM((32, 64, 256), F32),
        ],
        spaces={0: SM},
    )
    shares = lax.all_to_all(
        projected.reshape(8, 4, 16, 256), "det", split_axis=0, concat_axis=0, tiled=True
    )
    coupled = call(
        couple_kernel,
        (det_rank.astype(jnp.int32).reshape(1), shares, couple, couple_zero),
        [((4, 16, 256), F32)],
        spaces={0: SM},
    )
    coupled = lax.all_gather(coupled, "det", axis=0, tiled=True)

    filtered = call(
        columns_kernel,
        (rank, columns, *start, *middle, *end),
        [((128, 2048), F32)],
        [VM((16, 64, 256), F32), VM((16, 64, 256), F32)],
        spaces={0: SM},
    )
    returned_rows = lax.all_to_all(filtered, ("det", "tm"), split_axis=0, concat_axis=0, tiled=True)

    returned = call(
        clean_kernel,
        (
            slots, pointing.T.reshape(8, 512), coupled, spectrum, weight, weight_zero, mode_loading,
            beam_kernel, *turn, *behind,
        ),
        [((32, 32, 128), F32)],
        [
            VM((32, 64, 256), F32),
            VM((32, 64, 256), F32),
            VM((64, 64, 128), F32),
            VM((512, 512), BF16),
            VM((512, 256), F32),
        ],
        spaces={0: SM},
    )
    delivered = lax.all_to_all(returned, "tm", split_axis=0, concat_axis=0, tiled=True)
    prior = call(
        rows_back_kernel,
        (returned_rows, *turn, *behind),
        [((32, 8192), F32)],
        [VM((1024, 256), F32), VM((32, 32, 256), F32)],
    )
    return call(final_kernel, (asked, delivered, prior), [((32, 8192), F32)], spaces={0: SM})


def solution(mesh):
    return jax.shard_map(
        local,
        mesh=mesh,
        in_specs=(
            P("det", "tm"),
            P(("det", "tm"), None),
            P("det", "tm"),
            P(("det", "tm"), None),
            P(("det", "tm")),
            P(),
            P("det", None),
            P("det", None),
            P(),
        ),
        out_specs=P(("det", "tm"), None),
        check_vma=False,
    )
```

time: 623 us -> 141 us (0.23); the launches traced: 611 us -> 140 us
  matrix products: 257 us -> 0 us
  local copies, waits for them, and re-layouts: 164 us -> 19.3 us
  waiting for transfers between devices: 96.7 us -> 19.8 us
  other arithmetic: 42 us -> 0 us
  Pallas kernels: 0 us -> 35.3 us
  blocking collectives: 0 us -> 31.7 us
  between operations: 14.5 us -> 0.47 us
    dot_general x48 -> x0, matrix products: 251 us -> none  [the longest x1 110 us: couple_modes(): jnp.einsum('mnf,cnf->cmf', kernel_freq, projection, precision=precise)]
    psum x1 -> x0, waiting for transfers between devices: 63.2 us -> none  [local(): total_proj = lax.psum(local_proj, 'det')]
    gather x3 -> x0, local copies, waits for them, and re-layouts: 36.9 us -> none  [the longest x1 24.7 us: local(): row_index = (slot_index[list_slot] * rows_here + block_row).reshape(-1)]
    pallas_call x0 -> x10, Pallas kernels: none -> 35.3 us  [call(): pl.pallas_call(kernel, out_shape=shapes, in_specs=in_specs, out_specs=out...]
    dot_general x1 -> x0, local copies, waits for them, and re-layouts: 32.3 us -> none  [couple_modes(): jnp.einsum('bmn,bf->mnf', kernel, band_onehot, precision=precise)]
    reshape x11 -> x1, local copies, waits for them, and re-layouts: 28.2 us -> 0.08 us  [local(): pointing.T.reshape(8, 512)]
    scatter-add x2 -> x0, other arithmetic: 27.2 us -> none  [the longest x1 23.8 us: local(): returned = jnp.zeros_like(arrived_rows).at[row_index].add(row_grads)]
    all_to_all x2, waiting for transfers between devices: 24.8 us -> 3.64 us  [the longest x1 3.64 us: local(): lax.all_to_all(projected.reshape(8, 4, 16, 256), 'det', split_axis=0, con...]
  transfers between devices with their start and end apart: 6 -> 5, of which waited for: 3 -> 3; matrix products, arithmetic and copies ran while one was open for 71% -> 7% of each run, Pallas kernels for 0% -> 22%
where the time goes in v1:
time: 141 us; the launch traced here: 140 us
  Pallas kernels  35.3 us (25%)
  starting transfers between devices  33.5 us (24%)
  blocking collectives  31.7 us (22%)
  waiting for transfers between devices  19.8 us (14%)
  local copies, waits for them, and re-layouts  19.3 us (14%)
    pallas_call x10, Pallas kernels, call(): pl.pallas_call(kernel, out_shape=shapes, in_specs=in_specs, out_specs=out...  35.3 us
    all_gather x1, blocking collectives, local(): coupled = lax.all_gather(coupled, 'det', axis=0, tiled=True)  16.3 us
    all_to_all x1, blocking collectives, local(): asked = lax.all_to_all(send, 'tm', split_axis=0, concat_axis=0, tiled=True)  15.4 us
    unnamed x91, local copies, waits for them, and re-layouts  14.1 us
    all_to_all x1, starting transfers between devices, local(): lax.all_to_all(returned, 'tm', split_axis=0, concat_axis=0, tiled=True)  10.3 us
    all_to_all x1, waiting for transfers between devices, local(): lax.all_to_all(returned, 'tm', split_axis=0, concat_axis=0, tiled=True)  9.22 us
    all_to_all x1, starting transfers between devices, local(): lax.all_to_all(filtered, ('det', 'tm'), split_axis=0, concat_axis=0, tile...  9 us
    all_to_all x1, waiting for transfers between devices, local(): lax.all_to_all(outgoing, 'tm', split_axis=0, concat_axis=0, tiled=True)  6.96 us
  transfers between devices with their start and end apart: 5, of which 3 were waited for; matrix products, arithmetic and copies ran while one was open for 7% of the time, Pallas kernels for 22%

profile of v1, /device:TPU:0, one launch (start us, length us, event | category | flops | bytes accessed | tf_op | source)
XLA Modules:
  0.0 140.0 jit_solution(5767136853501671152)
XLA Ops:
  1.3 1.2 ids_kernel.1
  2.6 15.4 %all_to_all.48 = s32[16,1,128]{2,1,0:T(1,128)S(1)} all-to-all(s32[16,1,128]{2,1,0:T(1,128)S(1)} %bitcast.29), channel_id=1, replica_groups=mesh['det'=8,'tm'=16] {'tm'}, dimensions={0} | all-to-all | bytes 16384 | tf_op jit(solution)/shard_map/all_to_all | solution.py:540
  17.9 1.2 copy-done
  19.2 1.7 %pick_kernel.1 = f32[32,32,128]{2,1,0:T(8,128)} custom-call(s32[16,128]{1,0:T(8,128)S(1)} %bitcast.27, f32[32,8192]{1,0:T(8,128)S(1)} %copy-done), custom_call_target="tpu_custom_call" | custom-call | tf_op jit(solution)/shard_map/pick_kernel/pallas_call | solution.py:481
  20.8 3.6 %all-to-all-start.1 = ((f32[32,32,128]{2,1,0:T(8,128)}), f32[32,32,128]{2,1,0:T(8,128)S(1)}, u32[]{:S(2)}, u32[]{:S(2)}) async-start(f32[32,32,128]{2,1,0:T(8,128)} %pick_kernel.1), calls=%async_computation.1 | async-start | bytes 1048576 | tf_op jit(solution)/shard_map/all_to_all | solution.py:542
  24.5 1.3 rows_kernel.1
  25.8 2.0 %copy.49 = f32[128,1,2048]{2,1,0:T(1,128)} copy(f32[128,1,2048]{2,0,1:T(8,128)S(1)} %bitcast.23) | data formatting | bytes 2097152 | tf_op jit(solution)/shard_map/all_to_all | solution.py:550
  27.9 7.0 %all-to-all-done.1.arrived = f32[32,32,128]{2,1,0:T(8,128)S(1)} async-done(((f32[32,32,128]{2,1,0:T(8,128)}), f32[32,32,128]{2,1,0:T(8,128)S(1)}, u32[]{:S(2)}, u32[]{:S(2)}) %all-to-all-start.1) | async-done | bytes 524320 | tf_op jit(solution)/shard_map/all_to_all | solution.py:542
  34.8 6.8 %all-to-all-start.4 = ((f32[128,1,2048]{2,1,0:T(1,128)}), f32[128,1,2048]{2,1,0:T(1,128)}, u32[]{:S(2)}, u32[]{:S(2)}) async-start(f32[128,1,2048]{2,1,0:T(1,128)} %copy.49), calls=%async_computation.4 | async-start | bytes 2097152 | tf_op jit(solution)/shard_map/all_to_all | solution.py:550
  41.6 1.0 copy.45
  42.6 0.7 copy.46.inv_white
  43.5 0.8 copy-done.26
  44.2 0.7 copy-done.37
  45.0 0.7 copy-done.38
  47.4 0.8 copy-done.16
  48.1 12.3 %detect_kernel.1 = (f32[32,64,256]{2,1,0:T(8,128)S(1)}, f32[32,16,256]{2,1,0:T(8,128)}) custom-call(s32[16]{0:T(128)S(1)} %get-tuple-element.14.slots, s32[64,64]{1,0:T(8,128)S(1)} %copy-done.16, f32[64,8192]{1,0:T(8,128)S(1)} %copy-done.2, f32[32,32,128]{2,1,0:T(8,128)S(1)} %all-to-all-done.1.arrived, f32[128,128]{1,0:T(8,128)S(1)} %bitcast.25, ...), custom_call_target="tpu_custom_call" | custom-call | tf_op jit(solution)/shard_map/detect_kernel/pallas_call | solution.py:481
  60.5 1.3 copy-done.3
  61.9 3.8 %all-to-all-start.2 = ((f32[8,4,16,256]{3,2,1,0:T(8,128)}), f32[8,4,16,256]{3,2,1,0:T(8,128)S(1)}, u32[]{:S(2)}, u32[]{:S(2)}) async-start(f32[8,4,16,256]{3,2,1,0:T(8,128)} %bitcast.9), calls=%async_computation.2 | async-start | bytes 1048576 | tf_op jit(solution)/shard_map/all_to_all | solution.py:574
  65.8 1.6 %copy.56 = f32[128,1,2048]{2,0,1:T(8,128)S(1)} copy(f32[128,1,2048]{2,1,0:T(1,128)} %all-to-all-done.4) | data formatting | bytes 2097152
  67.5 2.9 %columns_kernel.1 = f32[128,2048]{1,0:T(8,128)S(1)} custom-call(s32[1]{0:T(128)} %bitcast.10.rank, f32[128,2048]{1,0:T(8,128)S(1)} %bitcast.20, bf16[128,128]{1,0:T(8,128)(2,1)S(1)} %copy-done.31, bf16[128,128]{1,0:T(8,128)(2,1)S(1)} %copy-done.32, f32[64,128]{1,0:T(8,128)S(1)} %copy-done.33, f32[64,128]{1,0:T(8,128)S(1)} %copy-done.34, ...), custom_call_target="tpu_custom_call" | custom-call | tf_op jit(solution)/shard_map/columns_kernel/pallas_call | solution.py:481
  70.4 2.0 %copy.50 = f32[128,1,2048]{2,1,0:T(1,128)} copy(f32[128,1,2048]{2,0,1:T(8,128)S(1)} %bitcast.21) | data formatting | bytes 2097152 | tf_op jit(solution)/shard_map/all_to_all | solution.py:592
  72.4 3.6 %all-to-all-done.2.shares = f32[8,4,16,256]{3,2,1,0:T(8,128)S(1)} async-done(((f32[8,4,16,256]{3,2,1,0:T(8,128)}), f32[8,4,16,256]{3,2,1,0:T(8,128)S(1)}, u32[]{:S(2)}, u32[]{:S(2)}) %all-to-all-start.2) | async-done | bytes 524320 | tf_op jit(solution)/shard_map/all_to_all | solution.py:574
  76.1 9.0 %all-to-all-start.5 = ((f32[128,1,2048]{2,1,0:T(1,128)}), f32[128,1,2048]{2,1,0:T(1,128)}, u32[]{:S(2)}, u32[]{:S(2)}) async-start(f32[128,1,2048]{2,1,0:T(1,128)} %copy.50), calls=%async_computation.5 | async-start | bytes 2097152 | tf_op jit(solution)/shard_map/all_to_all | solution.py:592
  85.2 0.9 copy-done.28
  86.2 0.9 copy-done.30
  87.2 16.3 %all_gather.3.coupled = f32[32,16,256]{2,1,0:T(8,128)S(1)} all-gather(f32[4,16,256]{2,1,0:T(8,128)S(1)} %couple_kernel.1), channel_id=1, replica_groups=mesh['det'=8,'tm'=16] {'det'}, dimensions={0}, use_global_device_ids=true | all-gather | bytes 589824 | tf_op jit(solution)/shard_map/all_gather | solution.py:583
  103.6 12.0 %clean_kernel.1 = f32[32,32,128]{2,1,0:T(8,128)} custom-call(s32[16]{0:T(128)S(1)} %get-tuple-element.14.slots, s32[8,512]{1,0:T(8,128)S(1)} %reshape.25.points, f32[32,16,256]{2,1,0:T(8,128)S(1)} %all_gather.3.coupled, f32[32,64,256]{2,1,0:T(8,128)S(1)} %copy-done.4, f32[64,128]{1,0:T(8,128)S(1)} %get-tuple-element.15.weight, ...), custom_call_target="tpu_custom_call" | custom-call | tf_op jit(solution)/shard_map/clean_kernel/pallas_call | solution.py:481
  115.6 10.3 %all-to-all-start.3 = ((f32[32,32,128]{2,1,0:T(8,128)}), f32[32,32,128]{2,1,0:T(8,128)S(1)}, u32[]{:S(2)}, u32[]{:S(2)}) async-start(f32[32,32,128]{2,1,0:T(8,128)} %clean_kernel.1), calls=%async_computation.3 | async-start | bytes 1048576 | tf_op jit(solution)/shard_map/all_to_all | solution.py:610
  125.9 1.6 %copy.55 = f32[128,1,2048]{2,0,1:T(8,128)S(1)} copy(f32[128,1,2048]{2,1,0:T(1,128)} %all-to-all-done.5) | data formatting | bytes 2097152
  127.4 1.3 rows_back_kernel.1.prior
  128.7 9.2 %all-to-all-done.3.delivered = f32[32,32,128]{2,1,0:T(8,128)S(1)} async-done(((f32[32,32,128]{2,1,0:T(8,128)}), f32[32,32,128]{2,1,0:T(8,128)S(1)}, u32[]{:S(2)}, u32[]{:S(2)}) %all-to-all-start.3) | async-done | bytes 524320 | tf_op jit(solution)/shard_map/all_to_all | solution.py:610
  137.9 2.1 %final_kernel.1 = f32[32,8192]{1,0:T(8,128)} custom-call(s32[16,128]{1,0:T(8,128)S(1)} %bitcast.28, f32[32,32,128]{2,1,0:T(8,128)S(1)} %all-to-all-done.3.delivered, f32[32,8192]{1,0:T(8,128)S(1)} %rows_back_kernel.1.prior), custom_call_target="tpu_custom_call" | custom-call | tf_op jit(solution)/shard_map/final_kernel/pallas_call | solution.py:481
  (86 shorter events, 3.7 us)
Async XLA Ops:
  0.0 24.4 %copy-start.14 = (f32[32,128]{1,0:T(8,128)S(1)}, f32[32,128]{1,0:T(8,128)}, u32[]{:S(2)}) copy-start(f32[32,128]{1,0:T(8,128)} %constant.63.clone.cos) | copy-start | bytes 49156
  0.0 24.4 %copy-start.15 = (f32[32,128]{1,0:T(8,128)S(1)}, f32[32,128]{1,0:T(8,128)}, u32[]{:S(2)}) copy-start(f32[32,128]{1,0:T(8,128)} %constant.64.clone.sin) | copy-start | bytes 49156
  19.2 5.3 %copy-start.12 = (bf16[256,256]{1,0:T(8,128)(2,1)S(1)}, bf16[256,256]{1,0:T(8,128)(2,1)}, u32[]{:S(2)}) copy-start(bf16[256,256]{1,0:T(8,128)(2,1)} %constant.68.clone.spe_l) | copy-start | bytes 393220
  20.8 14.0 %all-to-all-start.1 = ((f32[32,32,128]{2,1,0:T(8,128)}), f32[32,32,128]{2,1,0:T(8,128)S(1)}, u32[]{:S(2)}, u32[]{:S(2)}) async-start(f32[32,32,128]{2,1,0:T(8,128)} %pick_kernel.1), calls=%async_computation.1 | async-start | bytes 1048576 | tf_op jit(solution)/shard_map/all_to_all | solution.py:542
  25.8 16.8 %copy-start.41 = (f32[64,32]{0,1:T(8,128)S(1)}, f32[64,32]{0,1:T(8,128)}, u32[]{:S(2)}) copy-start(f32[64,32]{0,1:T(8,128)} %param.41) | copy-start | bytes 24580
  25.8 17.5 %copy-start.42 = (f32[64,16]{0,1:T(8,128)S(1)}, f32[64,16]{0,1:T(8,128)}, u32[]{:S(2)}) copy-start(f32[64,16]{0,1:T(8,128)} %param.42) | copy-start | bytes 12292
  25.8 17.6 %copy-start.13 = (f32[128,128]{1,0:T(8,128)S(1)}, f32[128,128]{1,0:T(8,128)}, u32[]{:S(2)}) copy-start(f32[128,128]{1,0:T(8,128)} %beam.1) | copy-start | bytes 196612
  25.8 21.6 %copy-start.2 = (f32[64,8192]{1,0:T(8,128)S(1)}, f32[64,8192]{1,0:T(8,128)}, u32[]{:S(2)}) copy-start(f32[64,8192]{1,0:T(8,128)} %data.1) | copy-start | bytes 6291460
  34.8 27.1 %all-to-all-start.4 = ((f32[128,1,2048]{2,1,0:T(1,128)}), f32[128,1,2048]{2,1,0:T(1,128)}, u32[]{:S(2)}, u32[]{:S(2)}) async-start(f32[128,1,2048]{2,1,0:T(1,128)} %copy.49), calls=%async_computation.4 | async-start | bytes 2097152 | tf_op jit(solution)/shard_map/all_to_all | solution.py:550
  61.8 5.5 %copy-start.18 = (bf16[256,256]{1,0:T(8,128)(2,1)S(1)}, bf16[256,256]{1,0:T(8,128)(2,1)}, u32[]{:S(2)}) copy-start(bf16[256,256]{1,0:T(8,128)(2,1)} %constant.75.clone.gen_h) | copy-start | bytes 393220
  61.8 5.5 %copy-start.19 = (bf16[256,256]{1,0:T(8,128)(2,1)S(1)}, bf16[256,256]{1,0:T(8,128)(2,1)}, u32[]{:S(2)}) copy-start(bf16[256,256]{1,0:T(8,128)(2,1)} %constant.76.clone.gen_l) | copy-start | bytes 393220
  61.8 5.5 %copy-start.20 = (bf16[256,256]{1,0:T(8,128)(2,1)S(1)}, bf16[256,256]{1,0:T(8,128)(2,1)}, u32[]{:S(2)}) copy-start(bf16[256,256]{1,0:T(8,128)(2,1)} %constant.77.clone.spe_h) | copy-start | bytes 393220
  61.8 5.6 %copy-start.21 = (bf16[256,256]{1,0:T(8,128)(2,1)S(1)}, bf16[256,256]{1,0:T(8,128)(2,1)}, u32[]{:S(2)}) copy-start(bf16[256,256]{1,0:T(8,128)(2,1)} %constant.78.clone.spe_l) | copy-start | bytes 393220
  61.8 5.6 %copy-start.22 = (bf16[256,256]{1,0:T(8,128)(2,1)S(1)}, bf16[256,256]{1,0:T(8,128)(2,1)}, u32[]{:S(2)}) copy-start(bf16[256,256]{1,0:T(8,128)(2,1)} %constant.79.clone.gent_h) | copy-start | bytes 393220
  61.8 5.6 %copy-start.23 = (bf16[256,256]{1,0:T(8,128)(2,1)S(1)}, bf16[256,256]{1,0:T(8,128)(2,1)}, u32[]{:S(2)}) copy-start(bf16[256,256]{1,0:T(8,128)(2,1)} %constant.80.clone.gent_l) | copy-start | bytes 393220
  61.8 5.6 %copy-start.24 = (bf16[256,256]{1,0:T(8,128)(2,1)S(1)}, bf16[256,256]{1,0:T(8,128)(2,1)}, u32[]{:S(2)}) copy-start(bf16[256,256]{1,0:T(8,128)(2,1)} %constant.81.clone.spet_h) | copy-start | bytes 393220
  61.8 5.6 %copy-start.25 = (bf16[256,256]{1,0:T(8,128)(2,1)S(1)}, bf16[256,256]{1,0:T(8,128)(2,1)}, u32[]{:S(2)}) copy-start(bf16[256,256]{1,0:T(8,128)(2,1)} %constant.82.clone.spet_l) | copy-start | bytes 393220
  61.9 5.6 %copy-start.31 = (bf16[128,128]{1,0:T(8,128)(2,1)S(1)}, bf16[128,128]{1,0:T(8,128)(2,1)}, u32[]{:S(2)}) copy-start(bf16[128,128]{1,0:T(8,128)(2,1)} %constant.71.clone.left_h) | copy-start | bytes 98308
  61.9 5.5 %copy-start.32 = (bf16[128,128]{1,0:T(8,128)(2,1)S(1)}, bf16[128,128]{1,0:T(8,128)(2,1)}, u32[]{:S(2)}) copy-start(bf16[128,128]{1,0:T(8,128)(2,1)} %constant.72.clone.left_l) | copy-start | bytes 98308
  61.9 5.5 %copy-start.33 = (f32[64,128]{1,0:T(8,128)S(1)}, f32[64,128]{1,0:T(8,128)}, u32[]{:S(2)}) copy-start(f32[64,128]{1,0:T(8,128)} %constant.73.clone.cos) | copy-start | bytes 98308
  61.9 5.5 %copy-start.34 = (f32[64,128]{1,0:T(8,128)S(1)}, f32[64,128]{1,0:T(8,128)}, u32[]{:S(2)}) copy-start(f32[64,128]{1,0:T(8,128)} %constant.74.clone.sin) | copy-start | bytes 98308
  61.9 5.5 %copy-start.35 = (bf16[128,128]{1,0:T(8,128)(2,1)S(1)}, bf16[128,128]{1,0:T(8,128)(2,1)}, u32[]{:S(2)}) copy-start(bf16[128,128]{1,0:T(8,128)(2,1)} %constant.83.clone.back_h) | copy-start | bytes 98308
  61.9 5.5 %copy-start.36 = (bf16[128,128]{1,0:T(8,128)(2,1)S(1)}, bf16[128,128]{1,0:T(8,128)(2,1)}, u32[]{:S(2)}) copy-start(bf16[128,128]{1,0:T(8,128)(2,1)} %constant.84.clone.back_l) | copy-start | bytes 98308
  61.9 14.1 %all-to-all-start.2 = ((f32[8,4,16,256]{3,2,1,0:T(8,128)}), f32[8,4,16,256]{3,2,1,0:T(8,128)S(1)}, u32[]{:S(2)}, u32[]{:S(2)}) async-start(f32[8,4,16,256]{3,2,1,0:T(8,128)} %bitcast.9), calls=%async_computation.2 | async-start | bytes 1048576 | tf_op jit(solution)/shard_map/all_to_all | solution.py:574
  70.4 14.7 %copy-start.17 = (s32[64,64]{1,0:T(8,128)S(1)}, s32[64,64]{1,0:T(8,128)}, u32[]{:S(2)}) copy-start(s32[64,64]{1,0:T(8,128)} %pointing.1) | copy-start | bytes 49156
  72.4 31.2 %copy-start.4 = (f32[32,64,256]{2,1,0:T(8,128)S(1)}, f32[32,64,256]{2,1,0:T(8,128)}, u32[]{:S(2)}) copy-start(f32[32,64,256]{2,1,0:T(8,128)} %copy-done.3) | copy-start | bytes 6291460
  72.4 31.2 %copy-start.5 = (bf16[256,256]{1,0:T(8,128)(2,1)S(1)}, bf16[256,256]{1,0:T(8,128)(2,1)}, u32[]{:S(2)}) copy-start(bf16[256,256]{1,0:T(8,128)(2,1)} %constant.85.clone.gent_h) | copy-start | bytes 393220
  72.4 31.2 %copy-start.6 = (bf16[256,256]{1,0:T(8,128)(2,1)S(1)}, bf16[256,256]{1,0:T(8,128)(2,1)}, u32[]{:S(2)}) copy-start(bf16[256,256]{1,0:T(8,128)(2,1)} %constant.86.clone.gent_l) | copy-start | bytes 393220
  72.4 31.2 %copy-start.7 = (bf16[256,256]{1,0:T(8,128)(2,1)S(1)}, bf16[256,256]{1,0:T(8,128)(2,1)}, u32[]{:S(2)}) copy-start(bf16[256,256]{1,0:T(8,128)(2,1)} %constant.87.clone.spet_h) | copy-start | bytes 393220
  72.4 31.2 %copy-start.8 = (bf16[256,256]{1,0:T(8,128)(2,1)S(1)}, bf16[256,256]{1,0:T(8,128)(2,1)}, u32[]{:S(2)}) copy-start(bf16[256,256]{1,0:T(8,128)(2,1)} %constant.88.clone.spet_l) | copy-start | bytes 393220
  76.1 39.5 %all-to-all-start.5 = ((f32[128,1,2048]{2,1,0:T(1,128)}), f32[128,1,2048]{2,1,0:T(1,128)}, u32[]{:S(2)}, u32[]{:S(2)}) async-start(f32[128,1,2048]{2,1,0:T(1,128)} %copy.50), calls=%async_computation.5 | async-start | bytes 2097152 | tf_op jit(solution)/shard_map/all_to_all | solution.py:592
  115.6 22.4 %all-to-all-start.3 = ((f32[32,32,128]{2,1,0:T(8,128)}), f32[32,32,128]{2,1,0:T(8,128)S(1)}, u32[]{:S(2)}, u32[]{:S(2)}) async-start(f32[32,32,128]{2,1,0:T(8,128)} %clean_kernel.1), calls=%async_computation.3 | async-start | bytes 1048576 | tf_op jit(solution)/shard_map/all_to_all | solution.py:610
  (16 other events, 31.2 us)

commit v2 on v1

--- a/solution.py
+++ b/solution.py
@@ -7,6 +7,7 @@
 from jax.experimental import pallas as pl
 from jax.experimental.pallas import tpu as pltpu
 from jax.sharding import PartitionSpec as P
+
 
 NBAND = 32
 F32 = jnp.float32
@@ -188,29 +189,41 @@
     send[...] = table
 
 
-def pick_kernel(asked, sky, out):
-    def step(i, carry):
-        for c in range(2):
-            block = jnp.minimum(asked[i, c], 63)
-            out[2 * i + c] = sky[:, aligned(block, 128)]
-        return carry
-
-    lax.fori_loop(0, 16, step, 0)
-
-
-def prep_kernel(inv_white, band, band_zero, kernel, weight, weight_zero, couple, couple_zero):
-    for source, onehot, out in (
-        (inv_white, band, weight),
-        (inv_white, band_zero, weight_zero),
-        (kernel, band, couple),
-        (kernel, band_zero, couple_zero),
-    ):
-        out[...] = jnp.dot(
-            source[...], onehot[...], precision=lax.Precision.HIGHEST, preferred_element_type=F32
-        )
-
-
-def rows_kernel(sky, cos, sin, gen_h, gen_l, spe_h, spe_l, out, work, done):
+def pick_kernel(asked, sky, out, sem):
+    copies = []
+    for i in range(32):
+        block = jnp.minimum(asked[i // 2, i % 2], 63)
+        copies.append(pltpu.make_async_copy(sky.at[:, aligned(block, 128)], out.at[i], sem.at[i]))
+        copies[-1].start()
+    for copy in copies:
+        copy.wait()
+
+
+def exact(source, onehot):
+    return jnp.dot(
+        source, onehot, precision=lax.Precision.HIGHEST, preferred_element_type=F32
+    )
+
+
+def tables_kernel(kernel, bands, out):
+    for part in range(2):
+        out[part] = exact(kernel[...], bands[part])
+
+
+def level_weights(inv_white, bands):
+    levels = inv_white[...].T
+    return exact(levels, bands[0]), exact(levels, bands[1])
+
+
+def point_pairs(pointing, turned):
+    wide = jnp.concatenate([pointing[...], pointing[...]], axis=0)
+    turned[...] = jnp.concatenate([wide, wide], axis=1).T
+    lane = lax.broadcasted_iota(jnp.int32, (32, 128), 1)
+    even, odd = turned[pl.ds(0, 32, stride=2), :], turned[pl.ds(1, 32, stride=2), :]
+    return jnp.where(lane < 64, even, odd)
+
+
+def rows_kernel(sky, turn, later, out, work, done):
     def tile(i, carry):
         rows = aligned(i, 8)
         values = [sky[rows, 128 * u : 128 * u + 128] for u in range(64)]
@@ -219,27 +232,28 @@
             work[k, rows, 0:128] = real
             work[k, rows, 128:256] = imag
 
-        forward_tile(values, cos, sin, store)
+        forward_tile(values, turn[0], turn[1], store)
         return carry
 
     lax.fori_loop(0, 4, tile, 0)
+    tables = later.wait()
     for q in range(2):
         chunk = work[16 * q : 16 * q + 16].reshape(512, 256)
-        done[512 * q : 512 * q + 512] = mm_right(chunk, gen_h[...], gen_l[...])
-    done[0:32] = mm_right(work[0], spe_h[...], spe_l[...])
+        done[512 * q : 512 * q + 512] = mm_right(chunk, tables[0], tables[1])
+    done[0:32] = mm_right(work[0], tables[2], tables[3])
     for t in range(8):
         for c in range(2):
             block = done[128 * t : 128 * t + 128, 128 * c : 128 * c + 128]
-            out[:, 1024 * c + 128 * t : 1024 * c + 128 * t + 128] = block.T
+            out[pl.ds(8 * c + t, 128, stride=16), :] = block.T
 
 
 def columns_kernel(
-    rank, data, left_h, left_l, cos, sin, gen_h, gen_l, spe_h, spe_l, gent_h, gent_l, spet_h, spet_l,
-    back_h, back_l, out, work, gained,
+    meta, data, turn, ends, later, out, work, gained,
 ):
+    cos, sin = turn.at[0], turn.at[1]
     for q in range(4):
-        lanes = slice(512 * q, 512 * q + 512)
-        both = mm_left(left_h[...], left_l[...], data[:, lanes])
+        block = [data[pl.ds(4 * q + s, 128, stride=16), :] for s in range(4)]
+        both = mm_left(ends[0], ends[1], jnp.concatenate(block, axis=1))
         for s in range(4):
             t = 4 * q + s
             real, imag = both[0:64, 128 * s : 128 * s + 128], both[64:128, 128 * s : 128 * s + 128]
@@ -256,15 +270,16 @@
         folded = jnp.minimum(vertical, total_rows - vertical).astype(F32) / total_rows
         squares.append(folded * folded)
     lane8 = lax.broadcasted_iota(jnp.int32, (8, 128), 1)
-    base = rank[0] * 64
+    base = meta[1] * 64
     knee_sq = 1.0 / (2.0 * math.pi * (total_rows / 64.0)) ** 2
     special = lax.broadcasted_iota(jnp.int32, (16, 8, 256), 1) == 0
+    tables = later.wait()
     for q in range(2):
         tiles = slice(8 * q, 8 * q + 8)
         gained[tiles] = mm_right(
-            work[tiles].reshape(512, 256), gen_h[...], gen_l[...]
+            work[tiles].reshape(512, 256), tables[0], tables[1]
         ).reshape(8, 64, 256)
-    zero = mm_right(work[:, 0:8, :].reshape(128, 256), spe_h[...], spe_l[...]).reshape(16, 8, 256)
+    zero = mm_right(work[:, 0:8, :].reshape(128, 256), tables[2], tables[3]).reshape(16, 8, 256)
     gained[:, 0:8, :] = jnp.where(special, zero, gained[:, 0:8, :])
 
     def gain_tile(t, carry):
@@ -284,9 +299,9 @@
     for q in range(2):
         tiles = slice(8 * q, 8 * q + 8)
         work[tiles] = mm_right(
-            gained[tiles].reshape(512, 256), gent_h[...], gent_l[...]
+            gained[tiles].reshape(512, 256), tables[4], tables[5]
         ).reshape(8, 64, 256)
-    zero = mm_right(gained[:, 0:8, :].reshape(128, 256), spet_h[...], spet_l[...])
+    zero = mm_right(gained[:, 0:8, :].reshape(128, 256), tables[6], tables[7])
     work[:, 0:8, :] = jnp.where(special, zero.reshape(16, 8, 256), work[:, 0:8, :])
     for q in range(4):
         pieces = []
@@ -297,19 +312,21 @@
                     [real * cos[...] - imag * sin[...], imag * cos[...] + real * sin[...]], axis=0
                 )
             )
-        both = jnp.concatenate(pieces, axis=1)
-        out[:, 512 * q : 512 * q + 512] = mm_left(back_h[...], back_l[...], both)
-
-
-def rows_back_kernel(data, cos, sin, gent_h, gent_l, spet_h, spet_l, out, work, done):
+        both = mm_left(ends[2], ends[3], jnp.concatenate(pieces, axis=1))
+        for s in range(4):
+            out[pl.ds(4 * q + s, 128, stride=16), :] = both[:, 128 * s : 128 * s + 128]
+
+
+def rows_back_kernel(data, turn, later, out, work, done):
     for t in range(8):
         for c in range(2):
-            block = data[:, 1024 * c + 128 * t : 1024 * c + 128 * t + 128]
+            block = data[pl.ds(8 * c + t, 128, stride=16), :]
             work[128 * t : 128 * t + 128, 128 * c : 128 * c + 128] = block.T
+    tables = later.wait()
     for q in range(2):
         chunk = work[512 * q : 512 * q + 512]
-        done[16 * q : 16 * q + 16] = mm_right(chunk, gent_h[...], gent_l[...]).reshape(16, 32, 256)
-    done[0] = mm_right(work[0:32], spet_h[...], spet_l[...])
+        done[16 * q : 16 * q + 16] = mm_right(chunk, tables[0], tables[1]).reshape(16, 32, 256)
+    done[0] = mm_right(work[0:32], tables[2], tables[3])
 
     def tile(i, carry):
         rows = aligned(i, 8)
@@ -317,7 +334,7 @@
         def load(k):
             return done[k, rows, 0:128], done[k, rows, 128:256]
 
-        values = inverse_tile(load, cos, sin)
+        values = inverse_tile(load, turn[0], turn[1])
         for u in range(64):
             out[rows, 128 * u : 128 * u + 128] = values[u]
         return carry
@@ -326,12 +343,13 @@
 
 
 def detect_kernel(
-    slots, pointing, data, arrived, beam_t, cos, sin, gen_h, gen_l, spe_h, spe_l, weight, weight_zero,
-    loading, spectrum, projected, points, picked, table, onehot, signal, work,
+    meta, slots, pointing, data_later, arrived, beam, turn, tables_later, inv_white, bands, loading_t,
+    spectrum_hbm, mine, theirs, points, picked, table, onehot, signal, work, spectrum, sem,
 ):
+    weight, weight_zero = level_weights(inv_white, bands)
     for i in range(16):
         picked[32 * i : 32 * i + 32] = arrived[slots[i]]
-    high, low = parts(mm_both(picked[...], beam_t[...]))
+    high, low = parts(mm_both(picked[...], beam[...].T))
     table[:, 0:128] = high
     table[:, 128:256] = low
     points[:, 0:64] = pointing[...]
@@ -348,6 +366,7 @@
         return carry
 
     lax.fori_loop(0, 8, gather, 0)
+    data = data_later.wait()
 
     def tile(i, carry):
         rows = aligned(i, 8)
@@ -357,70 +376,95 @@
             work[k, rows, 0:128] = real
             work[k, rows, 128:256] = imag
 
-        forward_tile(values, cos, sin, store)
+        forward_tile(values, turn[0], turn[1], store)
         return carry
 
     lax.fori_loop(0, 8, tile, 0)
+
+    tables = tables_later.wait()
 
     def stage(q, carry):
         chunk = work[aligned(q, 8)].reshape(512, 256)
-        spectrum[aligned(q, 8)] = mm_right(chunk, gen_h[...], gen_l[...]).reshape(8, 64, 256)
+        spectrum[aligned(q, 8)] = mm_right(chunk, tables[0], tables[1]).reshape(8, 64, 256)
         return carry
 
     lax.fori_loop(0, 4, stage, 0)
-    spectrum[0] = mm_right(work[0], spe_h[...], spe_l[...])
-    left_h, left_l = parts(loading[...].T)
-
-    def project(k, carry):
-        first = jnp.where(k == 0, weight_zero[...], weight[...])
-        scale = jnp.concatenate([first, weight[...]], axis=1)
-        projected[k] = mm_left(left_h, left_l, spectrum[k] * scale)
-        return carry
-
-    lax.fori_loop(0, 32, project, 0)
-
-
-def couple_kernel(place, shares, couple, couple_zero, out):
-    def one(k, carry):
-        total = shares[0, k]
-        for s in range(1, shares.shape[0]):
-            total = total + shares[s, k]
-        pick = (place[0] == 0) & (k == 0)
+    spectrum[0] = mm_right(work[0], tables[2], tables[3])
+    outward = pltpu.make_async_copy(spectrum, spectrum_hbm, sem)
+    outward.start()
+    left_h, left_l = parts(loading_t[...])
+    core = meta[3]
+
+    def project(i, carry):
+        for out, side in ((theirs, 1 - core), (mine, core)):
+            k = 8 * (i // 4) + 4 * side + i % 4
+            first = jnp.where(k == 0, weight_zero, weight)
+            scale = jnp.concatenate([first, weight], axis=1)
+            out[i] = mm_left(left_h, left_l, spectrum[k] * scale)
+        return carry
+
+    lax.fori_loop(0, 16, project, 0, unroll=4)
+    outward.wait()
+
+
+def merge_kernel(meta, mine, theirs, *outs):
+    for s in range(4):
+        rows = aligned((meta[2] + s) % 4, 4)
+        outs[s][...] = mine[rows] + theirs[rows]
+
+
+def couple_kernel(meta, own, one, two, three, couple, out):
+    for k in range(4):
+        total = (own[k] + one[k]) + (two[k] + three[k])
         real = jnp.zeros((16, 128), F32)
         imag = jnp.zeros((16, 128), F32)
         for n in range(16):
-            factor = couple[16 * n : 16 * n + 16]
-            first = jnp.where(pick, couple_zero[16 * n : 16 * n + 16], factor)
+            factor = couple[0, pl.ds(n, 16, stride=16), :]
+            first = factor
+            if k == 0:
+                first = jnp.where(meta[0] == 0, couple[1, pl.ds(n, 16, stride=16), :], factor)
             real = real + first * total[n : n + 1, 0:128]
             imag = imag + factor * total[n : n + 1, 128:256]
         out[k, :, 0:128] = real
         out[k, :, 128:256] = imag
-        return carry
-
-    lax.fori_loop(0, 4, one, 0)
 
 
 def clean_kernel(
-    slots, points, coupled, spectrum, weight, weight_zero, loading, beam, cos, sin, gent_h, gent_l,
-    spet_h, spet_l, out, filtered, work, cleaned, onehot, total,
+    meta, slots, pointing, a0, a1, a2, a3, b0, b1, b2, b3, spectrum_hbm, inv_white, bands, loading_t,
+    beam, turn, tables_later, out, filtered, work, cleaned, onehot, total, coupled, turned, points,
+    spectrum, sem,
 ):
-    left_h, left_l = parts(loading[...])
+    inward = []
+    for q in range(4):
+        rows = slice(8 * q, 8 * q + 8)
+        inward.append(pltpu.make_async_copy(spectrum_hbm.at[rows], spectrum.at[rows], sem.at[q]))
+        inward[-1].start()
+    for s, (here, there) in enumerate(((a0, b0), (a1, b1), (a2, b2), (a3, b3))):
+        chip = (meta[2] + (4 - s)) % 4
+        coupled[aligned(2 * chip + meta[3], 4)] = here[...]
+        coupled[aligned(2 * chip + 1 - meta[3], 4)] = there[...]
+    left_h, left_l = parts(loading_t[...].T)
+    points[...] = point_pairs(pointing, turned)
+    weight, weight_zero = level_weights(inv_white, bands)
 
     def remove(k, carry):
-        first = jnp.where(k == 0, weight_zero[...], weight[...])
-        scale = jnp.concatenate([first, weight[...]], axis=1)
+        first = jnp.where(k == 0, weight_zero, weight)
+        scale = jnp.concatenate([first, weight], axis=1)
         filtered[k] = scale * (spectrum[k] - mm_left(left_h, left_l, coupled[k]))
         return carry
 
-    lax.fori_loop(0, 32, remove, 0)
+    for copy in inward:
+        copy.wait()
+    lax.fori_loop(0, 32, remove, 0, unroll=4)
+    tables = tables_later.wait()
 
     def stage(q, carry):
         chunk = filtered[aligned(q, 8)].reshape(512, 256)
-        work[aligned(q, 8)] = mm_right(chunk, gent_h[...], gent_l[...]).reshape(8, 64, 256)
+        work[aligned(q, 8)] = mm_right(chunk, tables[0], tables[1]).reshape(8, 64, 256)
         return carry
 
     lax.fori_loop(0, 4, stage, 0)
-    work[0] = mm_right(filtered[0], spet_h[...], spet_l[...])
+    work[0] = mm_right(filtered[0], tables[2], tables[3])
 
     def tile(i, carry):
         rows = aligned(i, 8)
@@ -428,18 +472,19 @@
         def load(k):
             return work[k, rows, 0:128], work[k, rows, 128:256]
 
-        values = inverse_tile(load, cos, sin)
+        values = inverse_tile(load, turn[0], turn[1])
         for u in range(64):
             cleaned[u, rows, :] = values[u]
         return carry
 
     lax.fori_loop(0, 8, tile, 0)
-    sub = lax.broadcasted_iota(jnp.int32, (512, 512), 0)
+    sub = lax.broadcasted_iota(jnp.int32, (512, 128), 0)
     total[...] = jnp.zeros((512, 256), F32)
 
     def scatter(c, carry):
-        hit = points[pl.ds(c, 1), :] == sub
-        onehot[...] = jnp.where(hit, 1.0, 0.0).astype(BF16)
+        for u in range(4):
+            hit = points[pl.ds(4 * c + u, 1), :] == sub
+            onehot[:, 128 * u : 128 * u + 128] = jnp.where(hit, 1.0, 0.0).astype(BF16)
         high, low = parts(cleaned[aligned(c, 8)].reshape(512, 128))
         total[...] += mm(onehot[...], jnp.concatenate([high, low], axis=1))
         return carry
@@ -470,46 +515,91 @@
 
 
 SM = pltpu.SMEM
-
-
-def call(kernel, ins, outs, scratch=(), out_spaces=None, spaces=None):
-    spaces = spaces or {}
-    in_specs = [pl.BlockSpec(memory_space=spaces.get(i, VM)) for i in range(len(ins))]
-    out_spaces = out_spaces or [VM] * len(outs)
-    out_specs = [pl.BlockSpec(memory_space=s) for s in out_spaces]
-    shapes = [jax.ShapeDtypeStruct(s, d) for s, d in outs]
-    result = pl.pallas_call(
-        kernel,
+HBM = pltpu.HBM
+DMA = pltpu.SemaphoreType.DMA
+
+
+class Later:
+    def __init__(self, ref, copy):
+        self.ref, self.copy = ref, copy
+
+    def wait(self):
+        self.copy.wait()
+        return self.ref
+
+
+def call(kernel, modes, ins, outs, scratch=(), out_spaces=None, limit=24):
+    count, moved = len(ins), [i for i, m in enumerate(modes) if m in "etl"]
+    spaces = {"v": VM, "s": SM}
+    in_specs = [pl.BlockSpec(memory_space=spaces.get(m, HBM)) for m in modes]
+    out_specs = [pl.BlockSpec(memory_space=s) for s in (out_spaces or [VM] * len(outs))]
+    far = out_spaces or [VM] * len(outs)
+    shapes = [
+        HBM(s, d) if f is HBM else jax.ShapeDtypeStruct(s, d) for (s, d), f in zip(outs, far)
+    ]
+    buffers = [(SM if modes[i] == "t" else VM)(ins[i].shape, ins[i].dtype) for i in moved]
+
+    def body(*refs):
+        refs = list(refs)
+        if moved:
+            sems, targets = refs[-1], refs[-1 - len(moved) : -1]
+            copies = []
+            for n, (i, target) in enumerate(zip(moved, targets)):
+                copies.append(pltpu.make_async_copy(refs[i], target, sems.at[n]))
+                copies[-1].start()
+            for i, target, copy in zip(moved, targets, copies):
+                if modes[i] == "l":
+                    refs[i] = Later(target, copy)
+                else:
+                    copy.wait()
+                    refs[i] = target
+            refs = refs[: -1 - len(moved)]
+        kernel(*refs)
+
+    run = pl.pallas_call(
+        body,
         out_shape=shapes,
         in_specs=in_specs,
         out_specs=out_specs,
-        scratch_shapes=list(scratch),
-        compiler_params=pltpu.CompilerParams(vmem_limit_bytes=48 * 1024 * 1024),
-        name=kernel.__name__,
-    )(*ins)
+        scratch_shapes=list(scratch) + (buffers + [DMA((len(moved),))] if moved else []),
+        compiler_params=pltpu.CompilerParams(vmem_limit_bytes=limit * 1024 * 1024),
+    )
+    assert len(modes) == count
+    ins = [
+        pltpu.with_memory_space_constraint(x, HBM) if m in "hetl" else x for x, m in zip(ins, modes)
+    ]
+    result = run(*ins)
     return result if len(outs) > 1 else result[0]
 
 
 def row_constants():
     general, special = row_tables()
-    cos, sin = twiddles(32, np.arange(128), 8192)
+    turn = np.stack(twiddles(32, np.arange(128), 8192))
     scale = 2.0**-13
-    return (
-        (cos, sin),
-        (*halves(general), *halves(special)),
-        (*halves(general.T * scale), *halves(special.T * scale)),
-    )
+    ahead = np.stack([*halves(general), *halves(special)])
+    behind = np.stack([*halves(general.T * scale), *halves(special.T * scale)])
+    return turn, ahead, behind
 
 
 def col_constants():
     general, special = stage_tables(32, 4)
     left, back = real_left_table()
-    cos, sin = twiddles(64, np.arange(128) % 32, 4096)
-    return (
-        (*halves(left), cos, sin),
-        (*halves(general), *halves(special), *halves(general.T), *halves(special.T)),
-        halves(back * 2.0**-12),
-    )
+    turn = np.stack(twiddles(64, np.arange(128) % 32, 4096))
+    ends = np.stack([*halves(left), *halves(back * 2.0**-12)])
+    tables = np.stack([*halves(general), *halves(special), *halves(general.T), *halves(special.T)])
+    return turn, ends, tables
+
+
+def exchange(value, axes):
+    return lax.all_to_all(value, axes, split_axis=0, concat_axis=0, tiled=True)
+
+
+def core_swap(value):
+    return lax.ppermute(value, "det", [(g, g ^ 1) for g in range(8)])
+
+
+def chip_shift(value, step):
+    return lax.ppermute(value, "det", [(g, (g + 2 * step) % 8) for g in range(8)])
 
 
 def local(
@@ -523,98 +613,108 @@
     mode_loading,
     mode_kernel,
 ):
-    turn, ahead, behind = row_constants()
-    start, middle, end = col_constants()
-    band, band_zero = band_tables()
-    det_rank = lax.axis_index("det")
-    rank = (det_rank * lax.axis_size("tm") + lax.axis_index("tm")).astype(jnp.int32).reshape(1)
+    turn, ahead, behind = (jnp.asarray(t) for t in row_constants())
+    col_turn, ends, tables = (jnp.asarray(t) for t in col_constants())
+    bands = jnp.asarray(np.stack(band_tables()))
+    det = lax.axis_index("det").astype(jnp.int32)
+    rank = det * lax.axis_size("tm") + lax.axis_index("tm").astype(jnp.int32)
+    meta = jnp.stack([det, rank, det // 2, det % 2])
+    square, half = VM((32, 64, 256), F32), VM((32, 32, 256), F32)
+    flat = (32, 32, 128)
+    loading_t, inv_white = mode_loading.T, inv_white.T
 
     send, slots = call(
         ids_kernel,
+        "tt",
         (request_owner.reshape(16), request_block),
         [((16, 128), jnp.int32), ((16,), jnp.int32)],
         [SM((16,), jnp.int32)],
         [VM, SM],
-        {0: SM, 1: SM},
-    )
-    asked = lax.all_to_all(send, "tm", split_axis=0, concat_axis=0, tiled=True)
-    outgoing = call(pick_kernel, (asked, sky_map), [((32, 32, 128), F32)], spaces={0: SM})
-    arrived = lax.all_to_all(outgoing, "tm", split_axis=0, concat_axis=0, tiled=True)
-
+    )
+    asked = exchange(send, "tm")
+    outgoing = call(pick_kernel, "sh", (asked, sky_map), [(flat, F32)], [DMA((32,))])
+    arrived = exchange(outgoing, "tm")
+
+    wide = ((2048, 128), F32)
     packed = call(
-        rows_kernel,
-        (sky_map, *turn, *ahead),
-        [((128, 2048), F32)],
-        [VM((32, 32, 256), F32), VM((1024, 256), F32)],
-    )
-    columns = lax.all_to_all(packed, ("det", "tm"), split_axis=0, concat_axis=0, tiled=True)
-
-    weight, weight_zero, couple, couple_zero = call(
-        prep_kernel,
-        (inv_white, band, band_zero, mode_kernel.transpose(2, 1, 0).reshape(256, NBAND)),
-        [((64, 128), F32), ((64, 128), F32), ((256, 128), F32), ((256, 128), F32)],
-    )
-    spectrum, projected = call(
+        rows_kernel, "eel", (sky_map, turn, ahead), [wide], [half, VM((1024, 256), F32)]
+    )
+    columns = exchange(packed.reshape(128, 16, 128), ("det", "tm"))
+
+    spectrum, mine, theirs = call(
         detect_kernel,
+        "sselveeleee",
         (
-            slots, pointing, detector_data, arrived, beam_kernel.T, *turn, *ahead, weight, weight_zero,
-            mode_loading,
+            meta, slots, pointing, detector_data, arrived, beam_kernel, turn, ahead, inv_white, bands,
+            loading_t,
         ),
-        [((32, 64, 256), F32), ((32, 16, 256), F32)],
+        [((32, 64, 256), F32), ((16, 16, 256), F32), ((16, 16, 256), F32)],
         [
             VM((64, 128), jnp.int32),
             VM((512, 128), F32),
             VM((512, 256), BF16),
             VM((512, 512), BF16),
             VM((64, 64, 128), F32),
-            VM((32, 64, 256), F32),
+            square,
+            square,
+            DMA,
         ],
-        spaces={0: SM},
-    )
-    shares = lax.all_to_all(
-        projected.reshape(8, 4, 16, 256), "det", split_axis=0, concat_axis=0, tiled=True
-    )
-    coupled = call(
-        couple_kernel,
-        (det_rank.astype(jnp.int32).reshape(1), shares, couple, couple_zero),
-        [((4, 16, 256), F32)],
-        spaces={0: SM},
-    )
-    coupled = lax.all_gather(coupled, "det", axis=0, tiled=True)
+        [HBM, VM, VM],
+    )
+    share = ((4, 16, 256), F32)
+    partner = core_swap(theirs)
+    sums = call(merge_kernel, "svv", (meta, mine, partner), [share] * 4)
+    couple = call(
+        tables_kernel,
+        "ee",
+        (mode_kernel.transpose(1, 2, 0).reshape(256, NBAND), bands),
+        [((2, 256, 128), F32)],
+    )
+    gathered = [sums[0]] + [chip_shift(sums[s], s) for s in range(1, 4)]
+    coupled = call(couple_kernel, "svvvvv", (meta, *gathered, couple), [share])
+    here = [coupled] + [chip_shift(coupled, s) for s in range(1, 4)]
+    there = [core_swap(coupled)]
+    there += [core_swap(value) for value in here[1:]]
 
     filtered = call(
         columns_kernel,
-        (rank, columns, *start, *middle, *end),
-        [((128, 2048), F32)],
+        "sveel",
+        (meta, columns.reshape(2048, 128), col_turn, ends, tables),
+        [wide],
         [VM((16, 64, 256), F32), VM((16, 64, 256), F32)],
-        spaces={0: SM},
-    )
-    returned_rows = lax.all_to_all(filtered, ("det", "tm"), split_axis=0, concat_axis=0, tiled=True)
+    )
+    returned_rows = exchange(filtered.reshape(128, 16, 128), ("det", "tm"))
 
     returned = call(
         clean_kernel,
+        "sse" + "v" * 8 + "heeeeel",
         (
-            slots, pointing.T.reshape(8, 512), coupled, spectrum, weight, weight_zero, mode_loading,
-            beam_kernel, *turn, *behind,
+            meta, slots, pointing, *here, *there, spectrum, inv_white, bands, loading_t, beam_kernel,
+            turn, behind,
         ),
-        [((32, 32, 128), F32)],
+        [(flat, F32)],
         [
-            VM((32, 64, 256), F32),
-            VM((32, 64, 256), F32),
+            square,
+            square,
             VM((64, 64, 128), F32),
             VM((512, 512), BF16),
             VM((512, 256), F32),
+            VM((32, 16, 256), F32),
+            VM((128, 128), jnp.int32),
+            VM((32, 128), jnp.int32),
+            square,
+            DMA((4,)),
         ],
-        spaces={0: SM},
-    )
-    delivered = lax.all_to_all(returned, "tm", split_axis=0, concat_axis=0, tiled=True)
+    )
+    delivered = exchange(returned, "tm")
     prior = call(
         rows_back_kernel,
-        (returned_rows, *turn, *behind),
+        "vel",
+        (returned_rows.reshape(2048, 128), turn, behind),
         [((32, 8192), F32)],
-        [VM((1024, 256), F32), VM((32, 32, 256), F32)],
-    )
-    return call(final_kernel, (asked, delivered, prior), [((32, 8192), F32)], spaces={0: SM})
+        [VM((1024, 256), F32), half],
+    )
+    return call(final_kernel, "svv", (asked, delivered, prior), [((32, 8192), F32)])
 
 
 def solution(mesh):

time: 141 us -> 128 us (0.908)
  blocking collectives: 31.7 us -> 0 us
  waiting for transfers between devices: 19.8 us -> 43.8 us
  local copies, waits for them, and re-layouts: 19.3 us -> 0 us
  Pallas kernels: 35.3 us -> 42.8 us
  starting transfers between devices: 33.5 us -> 40.2 us
    all_gather x1 -> x0, blocking collectives: 16.3 us -> none  [local(): coupled = lax.all_gather(coupled, 'det', axis=0, tiled=True)]
    all_to_all x5, waiting for transfers between devices: 19.8 us -> 35.3 us  [exchange(): return lax.all_to_all(value, axes, split_axis=0, concat_axis=0, tiled=True)]
    all_to_all x1 -> x0, blocking collectives: 15.4 us -> none  [local(): asked = lax.all_to_all(send, 'tm', split_axis=0, concat_axis=0, tiled=True)]
    unnamed x91 -> x0, local copies, waits for them, and re-layouts: 14.1 us -> none
    ppermute x0 -> x11, starting transfers between devices: none -> 10.1 us  [the longest x6 9.37 us: chip_shift(): lax.ppermute(value, 'det', [(g, (g + 2 * step) % 8) for g in range(8)])]
    ppermute x0 -> x11, waiting for transfers between devices: none -> 8.48 us  [the longest x6 6.06 us: chip_shift(): lax.ppermute(value, 'det', [(g, (g + 2 * step) % 8) for g in range(8)])]
    pallas_call x10 -> x11, Pallas kernels: 35.3 us -> 42.8 us  [call(): result = run(*ins)]
    all_to_all x2 -> x0, local copies, waits for them, and re-layouts: 4.1 us -> none  [the longest x1 2.05 us: local(): lax.all_to_all(packed, ('det', 'tm'), split_axis=0, concat_axis=0, tiled=...]
  transfers between devices with their start and end apart: 5 -> 16, of which waited for: 3 -> 11; matrix products, arithmetic and copies ran while one was open for 7% -> 0% of each run, Pallas kernels for 22% -> 31%
where the time goes in v2:
time: 128 us; the launch traced here: 127 us
  waiting for transfers between devices  43.8 us (34%)
  Pallas kernels  42.8 us (33%)
  starting transfers between devices  40.2 us (31%)
    pallas_call x11, Pallas kernels, call(): result = run(*ins)  42.8 us
    all_to_all x5, waiting for transfers between devices, exchange(): return lax.all_to_all(value, axes, split_axis=0, concat_axis=0, tiled=True)  35.3 us
    all_to_all x5, starting transfers between devices, exchange(): return lax.all_to_all(value, axes, split_axis=0, concat_axis=0, tiled=True)  30.1 us
    ppermute x6, starting transfers between devices, chip_shift(): lax.ppermute(value, 'det', [(g, (g + 2 * step) % 8) for g in range(8)])  9.37 us
    ppermute x6, waiting for transfers between devices, chip_shift(): lax.ppermute(value, 'det', [(g, (g + 2 * step) % 8) for g in range(8)])  6.06 us
  transfers between devices with their start and end apart: 16, of which 11 were waited for; matrix products, arithmetic and copies ran while one was open for 0% of the time, Pallas kernels for 31%

profile of v2, /device:TPU:0, one launch (start us, length us, event | category | flops | bytes accessed | tf_op | source)
XLA Modules:
  0.0 127.0 jit_solution(7376679585751540159)
XLA Ops:
  0.0 1.4 %shard_map.154 = (s32[16,128]{1,0:T(8,128)}, s32[16]{0:T(128)S(1)}) custom-call(s32[16]{0:T(128)} %bitcast.27, s32[16]{0:T(128)} %refs_1_.5), custom_call_target="tpu_custom_call" | custom-call | tf_op jit(solution)/shard_map/pallas_call | solution.py:571
  1.4 8.0 %all-to-all-start = ((s32[16,1,128]{2,1,0:T(1,128)}), s32[16,1,128]{2,1,0:T(1,128)S(1)}, u32[]{:S(2)}, u32[]{:S(2)}) async-start(s32[16,1,128]{2,1,0:T(1,128)} %bitcast.2), calls=%async_computation | async-start | bytes 16384 | tf_op jit(solution)/shard_map/all_to_all | solution.py:594
  9.4 3.6 %shard_map.161 = f32[2048,128]{1,0:T(8,128)} custom-call(f32[32,8192]{1,0:T(8,128)} %refs_0_.1, f32[2,32,128]{2,1,0:T(8,128)} %constant.49.clone.refs_6_.refs_16_.refs_1_, bf16[4,256,256]{2,1,0:T(8,128)(2,1)} %constant.50.clone.refs_7_.refs_2_), custom_call_target="tpu_custom_call" | custom-call | tf_op jit(solution)/shard_map/pallas_call | solution.py:571
  13.0 3.9 %all-to-all-done = s32[16,1,128]{2,1,0:T(1,128)S(1)} async-done(((s32[16,1,128]{2,1,0:T(1,128)}), s32[16,1,128]{2,1,0:T(1,128)S(1)}, u32[]{:S(2)}, u32[]{:S(2)}) %all-to-all-start) | async-done | bytes 8224 | tf_op jit(solution)/shard_map/all_to_all | solution.py:594
  16.8 6.5 %all-to-all-start.3 = ((f32[128,16,128]{2,1,0:T(8,128)}), f32[128,16,128]{2,1,0:T(8,128)S(1)}, u32[]{:S(2)}, u32[]{:S(2)}) async-start(f32[128,16,128]{2,1,0:T(8,128)} %bitcast.12), calls=%async_computation.3 | async-start | bytes 2097152 | tf_op jit(solution)/shard_map/all_to_all | solution.py:594
  23.4 3.3 %shard_map.155 = f32[32,32,128]{2,1,0:T(8,128)} custom-call(s32[16,128]{1,0:T(8,128)S(1)} %bitcast.20, f32[32,8192]{1,0:T(8,128)} %refs_0_.1), custom_call_target="tpu_custom_call" | custom-call | tf_op jit(solution)/shard_map/pallas_call | solution.py:571
  26.7 15.7 %all-to-all-done.3 = f32[128,16,128]{2,1,0:T(8,128)S(1)} async-done(((f32[128,16,128]{2,1,0:T(8,128)}), f32[128,16,128]{2,1,0:T(8,128)S(1)}, u32[]{:S(2)}, u32[]{:S(2)}) %all-to-all-start.3) | async-done | bytes 1048608 | tf_op jit(solution)/shard_map/all_to_all | solution.py:594
  42.4 3.6 %all-to-all-start.1 = ((f32[32,32,128]{2,1,0:T(8,128)}), f32[32,32,128]{2,1,0:T(8,128)S(1)}, u32[]{:S(2)}, u32[]{:S(2)}) async-start(f32[32,32,128]{2,1,0:T(8,128)} %shard_map.155), calls=%async_computation.1 | async-start | bytes 1048576 | tf_op jit(solution)/shard_map/all_to_all | solution.py:594
  46.1 5.7 %shard_map.162 = f32[2048,128]{1,0:T(8,128)} custom-call(s32[4]{0:T(128)S(1)} %pad_add_fusion.refs_0_, f32[2048,128]{1,0:T(8,128)S(1)} %bitcast.18, f32[2,64,128]{2,1,0:T(8,128)} %constant.52.clone.refs_2_, bf16[4,128,128]{2,1,0:T(8,128)(2,1)} %constant.53.clone.refs_3_, bf16[8,256,256]{2,1,0:T(8,128)(2,1)} %constant.54.clone.refs_4_), custom_call_target="tpu_custom_call" | custom-call | tf_op jit(solution)/shard_map/pallas_call | solution.py:571
  51.8 6.0 %all-to-all-done.1.refs_4_ = f32[32,32,128]{2,1,0:T(8,128)S(1)} async-done(((f32[32,32,128]{2,1,0:T(8,128)}), f32[32,32,128]{2,1,0:T(8,128)S(1)}, u32[]{:S(2)}, u32[]{:S(2)}) %all-to-all-start.1) | async-done | bytes 524320 | tf_op jit(solution)/shard_map/all_to_all | solution.py:594
  57.7 4.6 %all-to-all-start.4 = ((f32[128,16,128]{2,1,0:T(8,128)}), f32[128,16,128]{2,1,0:T(8,128)S(1)}, u32[]{:S(2)}, u32[]{:S(2)}) async-start(f32[128,16,128]{2,1,0:T(8,128)} %bitcast.14), calls=%async_computation.4 | async-start | bytes 2097152 | tf_op jit(solution)/shard_map/all_to_all | solution.py:594
  62.3 10.2 %shard_map.156 = (f32[32,64,256]{2,1,0:T(8,128)}, f32[16,16,256]{2,1,0:T(8,128)S(1)}, f32[16,16,256]{2,1,0:T(8,128)S(1)}) custom-call(s32[4]{0:T(128)S(1)} %pad_add_fusion.refs_0_, s32[16]{0:T(128)S(1)} %get-tuple-element.15.refs_1_, s32[64,64]{1,0:T(8,128)} %refs_2_.6, f32[64,8192]{1,0:T(8,128)} %refs_3_.2, f32[32,32,128]{2,1,0:T(8,128)S(1)} %all-to-all-done.1.refs_4_, ...), custom_call_target="tpu_custom_call" | custom-call | tf_op jit(solution)/shard_map/pallas_call | solution.py:571
  72.7 1.5 %collective-permute-done.refs_2_ = f32[16,16,256]{2,1,0:T(8,128)S(1)} collective-permute-done((f32[16,16,256]{2,1,0:T(8,128)S(1)}, f32[16,16,256]{2,1,0:T(8,128)S(1)}, u32[]{:S(2)}, u32[]{:S(2)}) %collective-permute-start) | collective-permute-done | bytes 262176 | tf_op jit(solution)/shard_map/ppermute | solution.py:598
  74.2 0.6 shard_map.157
  74.8 0.9 collective-permute-start.1
  75.7 2.8 %collective-permute-start.2 = (f32[4,16,256]{2,1,0:T(8,128)S(1)}, f32[4,16,256]{2,1,0:T(8,128)S(1)}, u32[]{:S(2)}, u32[]{:S(2)}) collective-permute-start(f32[4,16,256]{2,1,0:T(8,128)S(1)} %get-tuple-element.20), channel_id=1, source_target_pairs={{0,64},{16,80},{32,96},{48,112},{64,0},{80,16},{96,32},{112,48},{1... | collective-permute-start | bytes 196616 | tf_op jit(solution)/shard_map/ppermute | solution.py:602
  78.5 1.4 %collective-permute-start.3 = (f32[4,16,256]{2,1,0:T(8,128)S(1)}, f32[4,16,256]{2,1,0:T(8,128)S(1)}, u32[]{:S(2)}, u32[]{:S(2)}) collective-permute-start(f32[4,16,256]{2,1,0:T(8,128)S(1)} %get-tuple-element.21), channel_id=1, source_target_pairs={{0,96},{16,112},{32,0},{48,16},{64,32},{80,48},{96,64},{112,80},{1... | collective-permute-start | bytes 196616 | tf_op jit(solution)/shard_map/ppermute | solution.py:602
  79.9 1.3 %shard_map.158.refs_5_ = f32[2,256,128]{2,1,0:T(8,128)S(1)} custom-call(f32[256,32]{1,0:T(8,128)} %bitcast.22, f32[2,32,128]{2,1,0:T(8,128)} %constant.55.clone.refs_9_.refs_1_.refs_13_), custom_call_target="tpu_custom_call" | custom-call | tf_op jit(solution)/shard_map/pallas_call | solution.py:571
  81.2 0.8 collective-permute-done.2.refs_3_
  82.0 0.8 collective-permute-done.3.refs_4_
  82.8 0.7 shard_map.159.refs_3_
  83.5 2.7 %collective-permute-start.6 = (f32[4,16,256]{2,1,0:T(8,128)S(1)}, f32[4,16,256]{2,1,0:T(8,128)S(1)}, u32[]{:S(2)}, u32[]{:S(2)}) collective-permute-start(f32[4,16,256]{2,1,0:T(8,128)S(1)} %shard_map.159.refs_3_), channel_id=1, source_target_pairs={{0,96},{16,112},{32,0},{48,16},{64,32},{80,48},{96,64},{112,80},{1... | collective-permute-start | bytes 196616 | tf_op jit(solution)/shard_map/ppermute | solution.py:602
  86.2 1.5 %collective-permute-start.5 = (f32[4,16,256]{2,1,0:T(8,128)S(1)}, f32[4,16,256]{2,1,0:T(8,128)S(1)}, u32[]{:S(2)}, u32[]{:S(2)}) collective-permute-start(f32[4,16,256]{2,1,0:T(8,128)S(1)} %shard_map.159.refs_3_), channel_id=1, source_target_pairs={{0,64},{16,80},{32,96},{48,112},{64,0},{80,16},{96,32},{112,48},{1... | collective-permute-start | bytes 196616 | tf_op jit(solution)/shard_map/ppermute | solution.py:602
  87.8 0.4 collective-permute-done.6.refs_6_
  88.3 4.1 %collective-permute-done.4.refs_4_ = f32[4,16,256]{2,1,0:T(8,128)S(1)} collective-permute-done((f32[4,16,256]{2,1,0:T(8,128)S(1)}, f32[4,16,256]{2,1,0:T(8,128)S(1)}, u32[]{:S(2)}, u32[]{:S(2)}) %collective-permute-start.4) | collective-permute-done | bytes 65568 | tf_op jit(solution)/shard_map/ppermute | solution.py:602
  92.4 0.5 collective-permute-start.9
  92.9 0.7 collective-permute-done.8.refs_8_
  93.8 11.7 %shard_map.160 = f32[32,32,128]{2,1,0:T(8,128)} custom-call(s32[4]{0:T(128)S(1)} %pad_add_fusion.refs_0_, s32[16]{0:T(128)S(1)} %get-tuple-element.15.refs_1_, s32[64,64]{1,0:T(8,128)} %refs_2_.6, f32[4,16,256]{2,1,0:T(8,128)S(1)} %shard_map.159.refs_3_, f32[4,16,256]{2,1,0:T(8,128)S(1)} %collective-permute-done.4.refs_4_, ...), custom_call_target="tpu_custom_call" | custom-call | tf_op jit(solution)/shard_map/pallas_call | solution.py:571
  105.5 7.3 %all-to-all-start.2 = ((f32[32,32,128]{2,1,0:T(8,128)}), f32[32,32,128]{2,1,0:T(8,128)S(1)}, u32[]{:S(2)}, u32[]{:S(2)}) async-start(f32[32,32,128]{2,1,0:T(8,128)} %shard_map.160), calls=%async_computation.2 | async-start | bytes 1048576 | tf_op jit(solution)/shard_map/all_to_all | solution.py:594
  112.9 2.3 %shard_map.163.refs_2_ = f32[32,8192]{1,0:T(8,128)S(1)} custom-call(f32[2048,128]{1,0:T(8,128)S(1)} %bitcast.19, f32[2,32,128]{2,1,0:T(8,128)} %constant.49.clone.refs_6_.refs_16_.refs_1_, bf16[4,256,256]{2,1,0:T(8,128)(2,1)} %constant.51.clone.refs_17_.refs_2_), custom_call_target="tpu_custom_call" | custom-call | tf_op jit(solution)/shard_map/pallas_call | solution.py:571
  115.2 9.7 %all-to-all-done.2.refs_1_ = f32[32,32,128]{2,1,0:T(8,128)S(1)} async-done(((f32[32,32,128]{2,1,0:T(8,128)}), f32[32,32,128]{2,1,0:T(8,128)S(1)}, u32[]{:S(2)}, u32[]{:S(2)}) %all-to-all-start.2) | async-done | bytes 524320 | tf_op jit(solution)/shard_map/all_to_all | solution.py:594
  124.9 2.1 %shard_map.164 = f32[32,8192]{1,0:T(8,128)} custom-call(s32[16,128]{1,0:T(8,128)S(1)} %bitcast.21, f32[32,32,128]{2,1,0:T(8,128)S(1)} %all-to-all-done.2.refs_1_, f32[32,8192]{1,0:T(8,128)S(1)} %shard_map.163.refs_2_), custom_call_target="tpu_custom_call" | custom-call | tf_op jit(solution)/shard_map/pallas_call | solution.py:571
  (12 shorter events, 0.5 us)
Async XLA Ops:
  1.4 15.4 %all-to-all-start = ((s32[16,1,128]{2,1,0:T(1,128)}), s32[16,1,128]{2,1,0:T(1,128)S(1)}, u32[]{:S(2)}, u32[]{:S(2)}) async-start(s32[16,1,128]{2,1,0:T(1,128)} %bitcast.2), calls=%async_computation | async-start | bytes 16384 | tf_op jit(solution)/shard_map/all_to_all | solution.py:594
  16.8 25.6 %all-to-all-start.3 = ((f32[128,16,128]{2,1,0:T(8,128)}), f32[128,16,128]{2,1,0:T(8,128)S(1)}, u32[]{:S(2)}, u32[]{:S(2)}) async-start(f32[128,16,128]{2,1,0:T(8,128)} %bitcast.12), calls=%async_computation.3 | async-start | bytes 2097152 | tf_op jit(solution)/shard_map/all_to_all | solution.py:594
  42.4 15.3 %all-to-all-start.1 = ((f32[32,32,128]{2,1,0:T(8,128)}), f32[32,32,128]{2,1,0:T(8,128)S(1)}, u32[]{:S(2)}, u32[]{:S(2)}) async-start(f32[32,32,128]{2,1,0:T(8,128)} %shard_map.155), calls=%async_computation.1 | async-start | bytes 1048576 | tf_op jit(solution)/shard_map/all_to_all | solution.py:594
  57.7 47.8 %all-to-all-start.4 = ((f32[128,16,128]{2,1,0:T(8,128)}), f32[128,16,128]{2,1,0:T(8,128)S(1)}, u32[]{:S(2)}, u32[]{:S(2)}) async-start(f32[128,16,128]{2,1,0:T(8,128)} %bitcast.14), calls=%async_computation.4 | async-start | bytes 2097152 | tf_op jit(solution)/shard_map/all_to_all | solution.py:594
  72.6 1.6 %collective-permute-start = (f32[16,16,256]{2,1,0:T(8,128)S(1)}, f32[16,16,256]{2,1,0:T(8,128)S(1)}, u32[]{:S(2)}, u32[]{:S(2)}) collective-permute-start(f32[16,16,256]{2,1,0:T(8,128)S(1)} %get-tuple-element.17), channel_id=1, source_target_pairs={{0,16},{16,0},{32,48},{48,32},{64,80},{80,64},{96,112},{112,96},{1... | collective-permute-start | bytes 786440 | tf_op jit(solution)/shard_map/ppermute | solution.py:598
  74.8 6.4 %collective-permute-start.1 = (f32[4,16,256]{2,1,0:T(8,128)S(1)}, f32[4,16,256]{2,1,0:T(8,128)S(1)}, u32[]{:S(2)}, u32[]{:S(2)}) collective-permute-start(f32[4,16,256]{2,1,0:T(8,128)S(1)} %get-tuple-element.19), channel_id=1, source_target_pairs={{0,32},{16,48},{32,64},{48,80},{64,96},{80,112},{96,0},{112,16},{1... | collective-permute-start | bytes 196616 | tf_op jit(solution)/shard_map/ppermute | solution.py:602
  75.7 6.3 %collective-permute-start.2 = (f32[4,16,256]{2,1,0:T(8,128)S(1)}, f32[4,16,256]{2,1,0:T(8,128)S(1)}, u32[]{:S(2)}, u32[]{:S(2)}) collective-permute-start(f32[4,16,256]{2,1,0:T(8,128)S(1)} %get-tuple-element.20), channel_id=1, source_target_pairs={{0,64},{16,80},{32,96},{48,112},{64,0},{80,16},{96,32},{112,48},{1... | collective-permute-start | bytes 196616 | tf_op jit(solution)/shard_map/ppermute | solution.py:602
  78.5 4.3 %collective-permute-start.3 = (f32[4,16,256]{2,1,0:T(8,128)S(1)}, f32[4,16,256]{2,1,0:T(8,128)S(1)}, u32[]{:S(2)}, u32[]{:S(2)}) collective-permute-start(f32[4,16,256]{2,1,0:T(8,128)S(1)} %get-tuple-element.21), channel_id=1, source_target_pairs={{0,96},{16,112},{32,0},{48,16},{64,32},{80,48},{96,64},{112,80},{1... | collective-permute-start | bytes 196616 | tf_op jit(solution)/shard_map/ppermute | solution.py:602
  83.5 4.6 %collective-permute-start.6 = (f32[4,16,256]{2,1,0:T(8,128)S(1)}, f32[4,16,256]{2,1,0:T(8,128)S(1)}, u32[]{:S(2)}, u32[]{:S(2)}) collective-permute-start(f32[4,16,256]{2,1,0:T(8,128)S(1)} %shard_map.159.refs_3_), channel_id=1, source_target_pairs={{0,96},{16,112},{32,0},{48,16},{64,32},{80,48},{96,64},{112,80},{1... | collective-permute-start | bytes 196616 | tf_op jit(solution)/shard_map/ppermute | solution.py:602
  86.2 6.2 %collective-permute-start.4 = (f32[4,16,256]{2,1,0:T(8,128)S(1)}, f32[4,16,256]{2,1,0:T(8,128)S(1)}, u32[]{:S(2)}, u32[]{:S(2)}) collective-permute-start(f32[4,16,256]{2,1,0:T(8,128)S(1)} %shard_map.159.refs_3_), channel_id=1, source_target_pairs={{0,32},{16,48},{32,64},{48,80},{64,96},{80,112},{96,0},{112,16},{1... | collective-permute-start | bytes 196616 | tf_op jit(solution)/shard_map/ppermute | solution.py:602
  86.2 6.2 %collective-permute-start.5 = (f32[4,16,256]{2,1,0:T(8,128)S(1)}, f32[4,16,256]{2,1,0:T(8,128)S(1)}, u32[]{:S(2)}, u32[]{:S(2)}) collective-permute-start(f32[4,16,256]{2,1,0:T(8,128)S(1)} %shard_map.159.refs_3_), channel_id=1, source_target_pairs={{0,64},{16,80},{32,96},{48,112},{64,0},{80,16},{96,32},{112,48},{1... | collective-permute-start | bytes 196616 | tf_op jit(solution)/shard_map/ppermute | solution.py:602
  87.8 5.2 %collective-permute-start.7 = (f32[4,16,256]{2,1,0:T(8,128)S(1)}, f32[4,16,256]{2,1,0:T(8,128)S(1)}, u32[]{:S(2)}, u32[]{:S(2)}) collective-permute-start(f32[4,16,256]{2,1,0:T(8,128)S(1)} %shard_map.159.refs_3_), channel_id=1, source_target_pairs={{0,16},{16,0},{32,48},{48,32},{64,80},{80,64},{96,112},{112,96},{1... | collective-permute-start | bytes 196616 | tf_op jit(solution)/shard_map/ppermute | solution.py:598
  88.1 4.8 %collective-permute-start.10 = (f32[4,16,256]{2,1,0:T(8,128)S(1)}, f32[4,16,256]{2,1,0:T(8,128)S(1)}, u32[]{:S(2)}, u32[]{:S(2)}) collective-permute-start(f32[4,16,256]{2,1,0:T(8,128)S(1)} %collective-permute-done.6.refs_6_), channel_id=1, source_target_pairs={{0,16},{16,0},{32,48},{48,32},{64,80},{80,64},{96,112},{112,96},{1... | collective-permute-start | bytes 196616 | tf_op jit(solution)/shard_map/ppermute | solution.py:598
  92.4 1.3 collective-permute-start.8
  92.4 1.4 %collective-permute-start.9 = (f32[4,16,256]{2,1,0:T(8,128)S(1)}, f32[4,16,256]{2,1,0:T(8,128)S(1)}, u32[]{:S(2)}, u32[]{:S(2)}) collective-permute-start(f32[4,16,256]{2,1,0:T(8,128)S(1)} %collective-permute-done.5.refs_5_), channel_id=1, source_target_pairs={{0,16},{16,0},{32,48},{48,32},{64,80},{80,64},{96,112},{112,96},{1... | collective-permute-start | bytes 196616 | tf_op jit(solution)/shard_map/ppermute | solution.py:598
  105.5 19.4 %all-to-all-start.2 = ((f32[32,32,128]{2,1,0:T(8,128)}), f32[32,32,128]{2,1,0:T(8,128)S(1)}, u32[]{:S(2)}, u32[]{:S(2)}) async-start(f32[32,32,128]{2,1,0:T(8,128)} %shard_map.160), calls=%async_computation.2 | async-start | bytes 1048576 | tf_op jit(solution)/shard_map/all_to_all | solution.py:594

commit v3 on v2

--- a/solution.py
+++ b/solution.py
@@ -49,17 +49,6 @@
         np.asarray(t, np.float32)
         for t in wave(np.arange(first, dtype=np.float64), second.astype(np.float64), length)
     ]
-
-
-def real_left_table():
-    index = np.arange(64, dtype=np.float64)
-    cos, sin = wave(index, np.arange(128, dtype=np.float64), 128)
-    forward = np.concatenate([cos, -sin], axis=0)
-    forward[64] = np.cos(math.pi * np.arange(128))
-    inverse = 2.0 * forward.T
-    inverse[:, 0] = 1.0
-    inverse[:, 64] = forward[64]
-    return forward, inverse
 
 
 def band_tables():
@@ -127,23 +116,24 @@
 
 
 def forward_tile(values, cos_ref, sin_ref, store):
+    half = len(values) // 2
     spectrum = real_transform(values)
-    store(0, spectrum[0][0], spectrum[32][0])
-    for k in range(1, 32):
+    store(0, spectrum[0][0], spectrum[half][0])
+    for k in range(1, half):
         real, imag = spectrum[k]
         cos, sin = cos_ref[k : k + 1, :], sin_ref[k : k + 1, :]
         store(k, real * cos + imag * sin, imag * cos - real * sin)
 
 
-def inverse_tile(load, cos_ref, sin_ref):
+def inverse_tile(load, cos_ref, sin_ref, half=32):
     first, last = load(0)
     spectrum = [(first, None)]
-    for k in range(1, 32):
+    for k in range(1, half):
         real, imag = load(k)
         cos, sin = cos_ref[k : k + 1, :], sin_ref[k : k + 1, :]
         spectrum.append((real * cos - imag * sin, imag * cos + real * sin))
     spectrum.append((last, None))
-    return real_inverse(spectrum, 64)
+    return real_inverse(spectrum, 2 * half)
 
 
 def parts(value):
@@ -205,11 +195,6 @@
     )
 
 
-def tables_kernel(kernel, bands, out):
-    for part in range(2):
-        out[part] = exact(kernel[...], bands[part])
-
-
 def level_weights(inv_white, bands):
     levels = inv_white[...].T
     return exact(levels, bands[0]), exact(levels, bands[1])
@@ -247,74 +232,76 @@
             out[pl.ds(8 * c + t, 128, stride=16), :] = block.T
 
 
-def columns_kernel(
-    meta, data, turn, ends, later, out, work, gained,
-):
-    cos, sin = turn.at[0], turn.at[1]
-    for q in range(4):
-        block = [data[pl.ds(4 * q + s, 128, stride=16), :] for s in range(4)]
-        both = mm_left(ends[0], ends[1], jnp.concatenate(block, axis=1))
-        for s in range(4):
-            t = 4 * q + s
-            real, imag = both[0:64, 128 * s : 128 * s + 128], both[64:128, 128 * s : 128 * s + 128]
-            work[t, :, 0:128] = real * cos[...] + imag * sin[...]
-            work[t, :, 128:256] = imag * cos[...] - real * sin[...]
+def columns_kernel(meta, data, turn, tables, out_hbm, work, gained, out, sems):
+    def ahead(i, carry):
+        tiles = aligned(i, 8)
+
+        def store(k, real, imag):
+            work[k, tiles, 0:128] = real
+            work[k, tiles, 128:256] = imag
+
+        forward_tile([data[d, tiles, :] for d in range(128)], turn[0], turn[1], store)
+        return carry
+
+    lax.fori_loop(0, 2, ahead, 0)
     total_rows, total_cols = 4096, 8192
-    row = lax.broadcasted_iota(jnp.int32, (64, 128), 0)
-    lane = lax.broadcasted_iota(jnp.int32, (64, 128), 1)
-    squares = []
-    for part in range(2):
-        vertical = row + 128 * (lane % 32)
-        if part:
-            vertical = jnp.where(row == 0, 64 + 128 * (lane % 32), vertical)
-        folded = jnp.minimum(vertical, total_rows - vertical).astype(F32) / total_rows
-        squares.append(folded * folded)
-    lane8 = lax.broadcasted_iota(jnp.int32, (8, 128), 1)
-    base = meta[1] * 64
+    tile = lax.broadcasted_iota(jnp.int32, (16, 128), 0)
+    lane = lax.broadcasted_iota(jnp.int32, (16, 128), 1)
+    first = 4 * (tile % 8) + lane // 32
+    first = jnp.where((first == 0) & (tile == 8), 32, first)
+    horizontal = meta[1] * 64 + first
+    lane_row = lax.broadcasted_iota(jnp.int32, (1, 128), 1)
+    folded = jnp.minimum(horizontal, total_cols - horizontal).astype(F32) / total_cols
+    across = folded * folded
     knee_sq = 1.0 / (2.0 * math.pi * (total_rows / 64.0)) ** 2
-    special = lax.broadcasted_iota(jnp.int32, (16, 8, 256), 1) == 0
-    tables = later.wait()
-    for q in range(2):
-        tiles = slice(8 * q, 8 * q + 8)
-        gained[tiles] = mm_right(
-            work[tiles].reshape(512, 256), tables[0], tables[1]
-        ).reshape(8, 64, 256)
-    zero = mm_right(work[:, 0:8, :].reshape(128, 256), tables[2], tables[3]).reshape(16, 8, 256)
-    gained[:, 0:8, :] = jnp.where(special, zero, gained[:, 0:8, :])
-
-    def gain_tile(t, carry):
-        first = 4 * (t % 8) + lane8 // 32
-        first = jnp.where((first == 0) & (t == 8), 32, first)
-        horizontal = base + first
-        folded = jnp.minimum(horizontal, total_cols - horizontal).astype(F32) / total_cols
-        across = (folded * folded)[0:1]
-        for part in range(2):
-            radial = squares[part] + across
-            gain = 1.0 + radial * (1.0 / 0.05) + 0.25 * lax.rsqrt(radial + knee_sq)
-            lanes = slice(128 * part, 128 * part + 128)
-            gained[t, :, lanes] = gained[t, :, lanes] * (-gain)
-        return carry
-
-    lax.fori_loop(0, 16, gain_tile, 0)
-    for q in range(2):
-        tiles = slice(8 * q, 8 * q + 8)
-        work[tiles] = mm_right(
-            gained[tiles].reshape(512, 256), tables[4], tables[5]
-        ).reshape(8, 64, 256)
-    zero = mm_right(gained[:, 0:8, :].reshape(128, 256), tables[6], tables[7])
-    work[:, 0:8, :] = jnp.where(special, zero.reshape(16, 8, 256), work[:, 0:8, :])
-    for q in range(4):
-        pieces = []
-        for s in range(4):
-            real, imag = work[4 * q + s, :, 0:128], work[4 * q + s, :, 128:256]
-            pieces.append(
-                jnp.concatenate(
-                    [real * cos[...] - imag * sin[...], imag * cos[...] + real * sin[...]], axis=0
-                )
-            )
-        both = mm_left(ends[2], ends[3], jnp.concatenate(pieces, axis=1))
-        for s in range(4):
-            out[pl.ds(4 * q + s, 128, stride=16), :] = both[:, 128 * s : 128 * s + 128]
+
+    def middle(q, carry):
+        chunk = work[aligned(q, 16)].reshape(256, 256)
+        gained[aligned(q, 16)] = mm_right(chunk, tables[0], tables[1]).reshape(16, 16, 256)
+
+        @pl.when(q == 0)
+        def _():
+            gained[0] = mm_right(work[0], tables[2], tables[3])
+
+        for j in range(16):
+            k = 16 * q + j
+            for part in range(2):
+                lead = jnp.where((k == 0) & (part == 1), 64, k)
+                vertical = lead + 128 * (lane_row % 32)
+                fold = jnp.minimum(vertical, total_rows - vertical).astype(F32) / total_rows
+                radial = fold * fold + across
+                gain = 1.0 + radial * (1.0 / 0.05) + 0.25 * lax.rsqrt(radial + knee_sq)
+                lanes = slice(128 * part, 128 * part + 128)
+                gained[k, :, lanes] = gained[k, :, lanes] * (-gain)
+        chunk = gained[aligned(q, 16)].reshape(256, 256)
+        work[aligned(q, 16)] = mm_right(chunk, tables[4], tables[5]).reshape(16, 16, 256)
+
+        @pl.when(q == 0)
+        def _():
+            work[0] = mm_right(gained[0], tables[6], tables[7])
+
+        return carry
+
+    lax.fori_loop(0, 4, middle, 0)
+
+    def outward(i):
+        return pltpu.make_async_copy(out.at[i], out_hbm.at[:, aligned(i, 8)], sems.at[i])
+
+    def behind(i, carry):
+        tiles = aligned(i, 8)
+
+        def load(k):
+            return work[k, tiles, 0:128], work[k, tiles, 128:256]
+
+        values = inverse_tile(load, turn[0], turn[1], 64)
+        for d in range(128):
+            out[i, d] = values[d]
+        outward(i).start()
+        return carry
+
+    lax.fori_loop(0, 2, behind, 0)
+    for i in range(2):
+        outward(i).wait()
 
 
 def rows_back_kernel(data, turn, later, out, work, done):
@@ -342,11 +329,28 @@
     lax.fori_loop(0, 4, tile, 0)
 
 
+def stage_kernel(
+    inv_white, bands, loading_t, kernel, pointing, *refs
+):
+    sources, targets = refs[:5], refs[5:10]
+    weights, couple, mixing, pairs, turned, sems = refs[10:]
+    copies = [pltpu.make_async_copy(a, b, sems.at[n]) for n, (a, b) in enumerate(zip(sources, targets))]
+    for copy in copies:
+        copy.start()
+    weights[0], weights[1] = level_weights(inv_white, bands)
+    for part in range(2):
+        couple[part] = exact(kernel[...], bands[part])
+    mixing[...] = loading_t[...].T
+    pairs[...] = point_pairs(pointing, turned)
+    for copy in copies:
+        copy.wait()
+
+
 def detect_kernel(
-    meta, slots, pointing, data_later, arrived, beam, turn, tables_later, inv_white, bands, loading_t,
-    spectrum_hbm, mine, theirs, points, picked, table, onehot, signal, work, spectrum, sem,
+    meta, slots, pointing, data_later, arrived, beam, turn, tables, weights, loading_t, spectrum_hbm, mine,
+    theirs, points, picked, table, onehot, signal, work, spectrum, sems,
 ):
-    weight, weight_zero = level_weights(inv_white, bands)
+    weight, weight_zero = weights[0], weights[1]
     for i in range(16):
         picked[32 * i : 32 * i + 32] = arrived[slots[i]]
     high, low = parts(mm_both(picked[...], beam[...].T))
@@ -357,9 +361,9 @@
     lane = lax.broadcasted_iota(jnp.int32, (64, 512), 1)
 
     def gather(c, carry):
-        turned = pltpu.roll(points[...], (128 - 8 * c) % 128, 1)
+        moved = pltpu.roll(points[...], (128 - 8 * c) % 128, 1)
         for u in range(8):
-            hit = turned[:, u : u + 1] == lane
+            hit = moved[:, u : u + 1] == lane
             onehot[64 * u : 64 * u + 64] = jnp.where(hit, 1.0, 0.0).astype(BF16)
         both = mm(onehot[...], table[...])
         signal[aligned(c, 8)] = (both[:, 0:128] + both[:, 128:256]).reshape(8, 64, 128)
@@ -381,17 +385,22 @@
 
     lax.fori_loop(0, 8, tile, 0)
 
-    tables = tables_later.wait()
+    def outward(q):
+        rows = aligned(q, 8)
+        return pltpu.make_async_copy(spectrum.at[rows], spectrum_hbm.at[rows], sems.at[q])
 
     def stage(q, carry):
         chunk = work[aligned(q, 8)].reshape(512, 256)
         spectrum[aligned(q, 8)] = mm_right(chunk, tables[0], tables[1]).reshape(8, 64, 256)
+
+        @pl.when(q == 0)
+        def _():
+            spectrum[0] = mm_right(work[0], tables[2], tables[3])
+
+        outward(q).start()
         return carry
 
     lax.fori_loop(0, 4, stage, 0)
-    spectrum[0] = mm_right(work[0], tables[2], tables[3])
-    outward = pltpu.make_async_copy(spectrum, spectrum_hbm, sem)
-    outward.start()
     left_h, left_l = parts(loading_t[...])
     core = meta[3]
 
@@ -404,7 +413,8 @@
         return carry
 
     lax.fori_loop(0, 16, project, 0, unroll=4)
-    outward.wait()
+    for q in range(4):
+        outward(q).wait()
 
 
 def merge_kernel(meta, mine, theirs, *outs):
@@ -430,22 +440,15 @@
 
 
 def clean_kernel(
-    meta, slots, pointing, a0, a1, a2, a3, b0, b1, b2, b3, spectrum_hbm, inv_white, bands, loading_t,
-    beam, turn, tables_later, out, filtered, work, cleaned, onehot, total, coupled, turned, points,
-    spectrum, sem,
+    meta, slots, pairs, a0, a1, a2, a3, b0, b1, b2, b3, spectrum_later, weights, mixing, beam, turn,
+    tables_later, out, filtered, work, cleaned, onehot, total, coupled,
 ):
-    inward = []
-    for q in range(4):
-        rows = slice(8 * q, 8 * q + 8)
-        inward.append(pltpu.make_async_copy(spectrum_hbm.at[rows], spectrum.at[rows], sem.at[q]))
-        inward[-1].start()
     for s, (here, there) in enumerate(((a0, b0), (a1, b1), (a2, b2), (a3, b3))):
         chip = (meta[2] + (4 - s)) % 4
         coupled[aligned(2 * chip + meta[3], 4)] = here[...]
         coupled[aligned(2 * chip + 1 - meta[3], 4)] = there[...]
-    left_h, left_l = parts(loading_t[...].T)
-    points[...] = point_pairs(pointing, turned)
-    weight, weight_zero = level_weights(inv_white, bands)
+    left_h, left_l = parts(mixing[...])
+    weight, weight_zero = weights[0], weights[1]
 
     def remove(k, carry):
         first = jnp.where(k == 0, weight_zero, weight)
@@ -453,8 +456,7 @@
         filtered[k] = scale * (spectrum[k] - mm_left(left_h, left_l, coupled[k]))
         return carry
 
-    for copy in inward:
-        copy.wait()
+    spectrum = spectrum_later.wait()
     lax.fori_loop(0, 32, remove, 0, unroll=4)
     tables = tables_later.wait()
 
@@ -483,7 +485,7 @@
 
     def scatter(c, carry):
         for u in range(4):
-            hit = points[pl.ds(4 * c + u, 1), :] == sub
+            hit = pairs[pl.ds(4 * c + u, 1), :] == sub
             onehot[:, 128 * u : 128 * u + 128] = jnp.where(hit, 1.0, 0.0).astype(BF16)
         high, low = parts(cleaned[aligned(c, 8)].reshape(512, 128))
         total[...] += mm(onehot[...], jnp.concatenate([high, low], axis=1))
@@ -517,6 +519,7 @@
 SM = pltpu.SMEM
 HBM = pltpu.HBM
 DMA = pltpu.SemaphoreType.DMA
+KEEP = "keep"
 
 
 class Later:
@@ -530,12 +533,15 @@
 
 def call(kernel, modes, ins, outs, scratch=(), out_spaces=None, limit=24):
     count, moved = len(ins), [i for i, m in enumerate(modes) if m in "etl"]
-    spaces = {"v": VM, "s": SM}
+    spaces = {"v": VM, "w": VM, "s": SM}
     in_specs = [pl.BlockSpec(memory_space=spaces.get(m, HBM)) for m in modes]
-    out_specs = [pl.BlockSpec(memory_space=s) for s in (out_spaces or [VM] * len(outs))]
+    out_specs = [
+        pl.BlockSpec(memory_space=VM if s is KEEP else s) for s in (out_spaces or [VM] * len(outs))
+    ]
     far = out_spaces or [VM] * len(outs)
     shapes = [
-        HBM(s, d) if f is HBM else jax.ShapeDtypeStruct(s, d) for (s, d), f in zip(outs, far)
+        (VM if f is KEEP else HBM)(s, d) if f in (HBM, KEEP) else jax.ShapeDtypeStruct(s, d)
+        for (s, d), f in zip(outs, far)
     ]
     buffers = [(SM if modes[i] == "t" else VM)(ins[i].shape, ins[i].dtype) for i in moved]
 
@@ -546,7 +552,10 @@
             copies = []
             for n, (i, target) in enumerate(zip(moved, targets)):
                 copies.append(pltpu.make_async_copy(refs[i], target, sems.at[n]))
-                copies[-1].start()
+            for kind in ("et", "l"):
+                for i, copy in zip(moved, copies):
+                    if modes[i] in kind:
+                        copy.start()
             for i, target, copy in zip(moved, targets, copies):
                 if modes[i] == "l":
                     refs[i] = Later(target, copy)
@@ -566,7 +575,8 @@
     )
     assert len(modes) == count
     ins = [
-        pltpu.with_memory_space_constraint(x, HBM) if m in "hetl" else x for x, m in zip(ins, modes)
+        pltpu.with_memory_space_constraint(x, VM if m == "w" else HBM) if m in "hetlw" else x
+        for x, m in zip(ins, modes)
     ]
     result = run(*ins)
     return result if len(outs) > 1 else result[0]
@@ -583,11 +593,10 @@
 
 def col_constants():
     general, special = stage_tables(32, 4)
-    left, back = real_left_table()
     turn = np.stack(twiddles(64, np.arange(128) % 32, 4096))
-    ends = np.stack([*halves(left), *halves(back * 2.0**-12)])
-    tables = np.stack([*halves(general), *halves(special), *halves(general.T), *halves(special.T)])
-    return turn, ends, tables
+    scale = 2.0**-12
+    behind = (*halves(general.T * scale), *halves(special.T * scale))
+    return turn, np.stack([*halves(general), *halves(special), *behind])
 
 
 def exchange(value, axes):
@@ -614,7 +623,7 @@
     mode_kernel,
 ):
     turn, ahead, behind = (jnp.asarray(t) for t in row_constants())
-    col_turn, ends, tables = (jnp.asarray(t) for t in col_constants())
+    col_turn, tables = (jnp.asarray(t) for t in col_constants())
     bands = jnp.asarray(np.stack(band_tables()))
     det = lax.axis_index("det").astype(jnp.int32)
     rank = det * lax.axis_size("tm") + lax.axis_index("tm").astype(jnp.int32)
@@ -641,13 +650,28 @@
     )
     columns = exchange(packed.reshape(128, 16, 128), ("det", "tm"))
 
+    moved = (turn, ahead, beam_kernel, col_turn, tables)
+    turn_v, ahead_v, beam_v, col_turn_v, tables_v, weights, couple, mixing, pairs = call(
+        stage_kernel,
+        "eeeeehhhhh",
+        (
+            inv_white, bands, loading_t, mode_kernel.transpose(1, 2, 0).reshape(256, NBAND), pointing,
+            *moved,
+        ),
+        [(m.shape, m.dtype) for m in moved]
+        + [
+            ((2, 64, 128), F32),
+            ((2, 256, 128), F32),
+            ((64, 16), F32),
+            ((32, 128), jnp.int32),
+        ],
+        [VM((128, 128), jnp.int32), DMA((5,))],
+        [KEEP] * 9,
+    )
     spectrum, mine, theirs = call(
         detect_kernel,
-        "sselveeleee",
-        (
-            meta, slots, pointing, detector_data, arrived, beam_kernel, turn, ahead, inv_white, bands,
-            loading_t,
-        ),
+        "sselvwwwwe",
+        (meta, slots, pointing, detector_data, arrived, beam_v, turn_v, ahead_v, weights, loading_t),
         [((32, 64, 256), F32), ((16, 16, 256), F32), ((16, 16, 256), F32)],
         [
             VM((64, 128), jnp.int32),
@@ -657,41 +681,32 @@
             VM((64, 64, 128), F32),
             square,
             square,
-            DMA,
+            DMA((4,)),
         ],
         [HBM, VM, VM],
     )
     share = ((4, 16, 256), F32)
     partner = core_swap(theirs)
     sums = call(merge_kernel, "svv", (meta, mine, partner), [share] * 4)
-    couple = call(
-        tables_kernel,
-        "ee",
-        (mode_kernel.transpose(1, 2, 0).reshape(256, NBAND), bands),
-        [((2, 256, 128), F32)],
-    )
     gathered = [sums[0]] + [chip_shift(sums[s], s) for s in range(1, 4)]
-    coupled = call(couple_kernel, "svvvvv", (meta, *gathered, couple), [share])
+    coupled = call(couple_kernel, "svvvvw", (meta, *gathered, couple), [share])
     here = [coupled] + [chip_shift(coupled, s) for s in range(1, 4)]
-    there = [core_swap(coupled)]
-    there += [core_swap(value) for value in here[1:]]
+    there = [core_swap(value) for value in here]
 
     filtered = call(
         columns_kernel,
-        "sveel",
-        (meta, columns.reshape(2048, 128), col_turn, ends, tables),
-        [wide],
-        [VM((16, 64, 256), F32), VM((16, 64, 256), F32)],
-    )
-    returned_rows = exchange(filtered.reshape(128, 16, 128), ("det", "tm"))
+        "svww",
+        (meta, columns, col_turn_v, tables_v),
+        [((128, 16, 128), F32)],
+        [VM((64, 16, 256), F32), VM((64, 16, 256), F32), VM((2, 128, 8, 128), F32), DMA((2,))],
+        [HBM],
+    )
+    returned_rows = exchange(filtered, ("det", "tm"))
 
     returned = call(
         clean_kernel,
-        "sse" + "v" * 8 + "heeeeel",
-        (
-            meta, slots, pointing, *here, *there, spectrum, inv_white, bands, loading_t, beam_kernel,
-            turn, behind,
-        ),
+        "ssw" + "v" * 8 + "lwwwwl",
+        (meta, slots, pairs, *here, *there, spectrum, weights, mixing, beam_v, turn_v, behind),
         [(flat, F32)],
         [
             square,
@@ -700,17 +715,13 @@
             VM((512, 512), BF16),
             VM((512, 256), F32),
             VM((32, 16, 256), F32),
-            VM((128, 128), jnp.int32),
-            VM((32, 128), jnp.int32),
-            square,
-            DMA((4,)),
         ],
     )
     delivered = exchange(returned, "tm")
     prior = call(
         rows_back_kernel,
-        "vel",
-        (returned_rows.reshape(2048, 128), turn, behind),
+        "vwl",
+        (returned_rows.reshape(2048, 128), turn_v, behind),
         [((32, 8192), F32)],
         [VM((1024, 256), F32), half],
     )

time: 128 us -> 125 us (0.977)
  starting transfers between devices: 40.2 us -> 38.7 us
    all_to_all x5, waiting for transfers between devices: 35.3 us -> 32.7 us  [exchange(): return lax.all_to_all(value, axes, split_axis=0, concat_axis=0, tiled=True)]
    ppermute x6, waiting for transfers between devices: 6.06 us -> 8.36 us  [chip_shift(): lax.ppermute(value, 'det', [(g, (g + 2 * step) % 8) for g in range(8)])]
  transfers between devices with their start and end apart: 16 -> 16, of which waited for: 11 -> 13; matrix products, arithmetic and copies ran while one was open for 0% -> 0% of each run, Pallas kernels for 31% -> 31%
where the time goes in v3:
time: 125 us
  waiting for transfers between devices  43.9 us (35%)
  Pallas kernels  41.9 us (34%)
  starting transfers between devices  38.7 us (31%)
    pallas_call x11, Pallas kernels, call(): result = run(*ins)  41.9 us
    all_to_all x5, waiting for transfers between devices, exchange(): return lax.all_to_all(value, axes, split_axis=0, concat_axis=0, tiled=True)  32.7 us
    all_to_all x5, starting transfers between devices, exchange(): return lax.all_to_all(value, axes, split_axis=0, concat_axis=0, tiled=True)  29.8 us
    ppermute x6, starting transfers between devices, chip_shift(): lax.ppermute(value, 'det', [(g, (g + 2 * step) % 8) for g in range(8)])  8.81 us
    ppermute x6, waiting for transfers between devices, chip_shift(): lax.ppermute(value, 'det', [(g, (g + 2 * step) % 8) for g in range(8)])  8.36 us
    ppermute x5, waiting for transfers between devices, core_swap(): return lax.ppermute(value, 'det', [(g, g ^ 1) for g in range(8)])  2.77 us
  transfers between devices with their start and end apart: 16, of which 13 were waited for; matrix products, arithmetic and copies ran while one was open for 0% of the time, Pallas kernels for 31%

profile of v3, /device:TPU:0, one launch (start us, length us, event | category | flops | bytes accessed | tf_op | source)
XLA Modules:
  0.0 124.6 jit_solution(11343213524458107599)
XLA Ops:
  0.0 1.4 %shard_map.145 = (s32[16,128]{1,0:T(8,128)}, s32[16]{0:T(128)S(1)}) custom-call(s32[16]{0:T(128)} %bitcast.23, s32[16]{0:T(128)} %refs_1_.4), custom_call_target="tpu_custom_call" | custom-call | tf_op jit(solution)/shard_map/pallas_call | solution.py:581
  1.4 8.0 %all-to-all-start = ((s32[16,1,128]{2,1,0:T(1,128)}), s32[16,1,128]{2,1,0:T(1,128)S(1)}, u32[]{:S(2)}, u32[]{:S(2)}) async-start(s32[16,1,128]{2,1,0:T(1,128)} %bitcast.2), calls=%async_computation | async-start | bytes 16384 | tf_op jit(solution)/shard_map/all_to_all | solution.py:603
  9.4 3.6 %shard_map.152 = f32[2048,128]{1,0:T(8,128)} custom-call(f32[32,8192]{1,0:T(8,128)} %refs_0_.1, f32[2,32,128]{2,1,0:T(8,128)} %constant.47.clone.refs_5_.refs_1_, bf16[4,256,256]{2,1,0:T(8,128)(2,1)} %constant.48.clone.refs_6_.refs_2_), custom_call_target="tpu_custom_call" | custom-call | tf_op jit(solution)/shard_map/pallas_call | solution.py:581
  13.0 4.0 %all-to-all-done = s32[16,1,128]{2,1,0:T(1,128)S(1)} async-done(((s32[16,1,128]{2,1,0:T(1,128)}), s32[16,1,128]{2,1,0:T(1,128)S(1)}, u32[]{:S(2)}, u32[]{:S(2)}) %all-to-all-start) | async-done | bytes 8224 | tf_op jit(solution)/shard_map/all_to_all | solution.py:603
  17.0 6.4 %all-to-all-start.3 = ((f32[128,16,128]{2,1,0:T(8,128)}), f32[128,16,128]{2,1,0:T(8,128)S(1)}, u32[]{:S(2)}, u32[]{:S(2)}) async-start(f32[128,16,128]{2,1,0:T(8,128)} %bitcast.12), calls=%async_computation.3 | async-start | bytes 2097152 | tf_op jit(solution)/shard_map/all_to_all | solution.py:603
  23.4 3.3 %shard_map.147 = f32[32,32,128]{2,1,0:T(8,128)} custom-call(s32[16,128]{1,0:T(8,128)S(1)} %bitcast.17, f32[32,8192]{1,0:T(8,128)} %refs_0_.1), custom_call_target="tpu_custom_call" | custom-call | tf_op jit(solution)/shard_map/pallas_call | solution.py:581
  26.7 15.7 %all-to-all-done.3.refs_1_ = f32[128,16,128]{2,1,0:T(8,128)S(1)} async-done(((f32[128,16,128]{2,1,0:T(8,128)}), f32[128,16,128]{2,1,0:T(8,128)S(1)}, u32[]{:S(2)}, u32[]{:S(2)}) %all-to-all-start.3) | async-done | bytes 1048608 | tf_op jit(solution)/shard_map/all_to_all | solution.py:603
  42.4 3.6 %all-to-all-start.1 = ((f32[32,32,128]{2,1,0:T(8,128)}), f32[32,32,128]{2,1,0:T(8,128)S(1)}, u32[]{:S(2)}, u32[]{:S(2)}) async-start(f32[32,32,128]{2,1,0:T(8,128)} %shard_map.147), calls=%async_computation.1 | async-start | bytes 1048576 | tf_op jit(solution)/shard_map/all_to_all | solution.py:603
  46.0 2.8 %shard_map.146 = (f32[2,32,128]{2,1,0:T(8,128)S(1)}, bf16[4,256,256]{2,1,0:T(8,128)(2,1)S(1)}, f32[128,128]{1,0:T(8,128)S(1)}, f32[2,64,128]{2,1,0:T(8,128)S(1)}...) custom-call(f32[32,64]{1,0:T(8,128)} %bitcast.22, ...), custom_call_target="tpu_custom_call" | custom-call | tf_op jit(solution)/shard_map/pallas_call | solution.py:581
  48.8 5.4 %shard_map.153 = f32[128,16,128]{2,1,0:T(8,128)} custom-call(s32[4]{0:T(128)S(1)} %pad_add_fusion.refs_0_, f32[128,16,128]{2,1,0:T(8,128)S(1)} %all-to-all-done.3.refs_1_, f32[2,64,128]{2,1,0:T(8,128)S(1)} %get-tuple-element.39.refs_2_, bf16[8,256,256]{2,1,0:T(8,128)(2,1)S(1)} %get-tuple-element.40.refs_3_), custom_call_target="tpu_custom_call" | custom-call | tf_op jit(solution)/shard_map/pallas_call | solution.py:581
  54.2 3.5 %all-to-all-done.1.refs_4_ = f32[32,32,128]{2,1,0:T(8,128)S(1)} async-done(((f32[32,32,128]{2,1,0:T(8,128)}), f32[32,32,128]{2,1,0:T(8,128)S(1)}, u32[]{:S(2)}, u32[]{:S(2)}) %all-to-all-start.1) | async-done | bytes 524320 | tf_op jit(solution)/shard_map/all_to_all | solution.py:603
  57.7 4.8 %all-to-all-start.4 = ((f32[128,16,128]{2,1,0:T(8,128)}), f32[128,16,128]{2,1,0:T(8,128)S(1)}, u32[]{:S(2)}, u32[]{:S(2)}) async-start(f32[128,16,128]{2,1,0:T(8,128)} %shard_map.153), calls=%async_computation.4 | async-start | bytes 2097152 | tf_op jit(solution)/shard_map/all_to_all | solution.py:603
  62.5 9.0 %shard_map.148 = (f32[32,64,256]{2,1,0:T(8,128)}, f32[16,16,256]{2,1,0:T(8,128)S(1)}, f32[16,16,256]{2,1,0:T(8,128)S(1)}) custom-call(s32[4]{0:T(128)S(1)} %pad_add_fusion.refs_0_, s32[16]{0:T(128)S(1)} %get-tuple-element.24.refs_1_, s32[64,64]{1,0:T(8,128)} %refs_2_.3, f32[64,8192]{1,0:T(8,128)} %refs_3_.1, f32[32,32,128]{2,1,0:T(8,128)S(1)} %all-to-all-done.1.refs_4_, ...), custom_call_target="tpu_custom_call" | custom-call | tf_op jit(solution)/shard_map/pallas_call | solution.py:581
  71.6 1.5 %collective-permute-done.refs_2_ = f32[16,16,256]{2,1,0:T(8,128)S(1)} collective-permute-done((f32[16,16,256]{2,1,0:T(8,128)S(1)}, f32[16,16,256]{2,1,0:T(8,128)S(1)}, u32[]{:S(2)}, u32[]{:S(2)}) %collective-permute-start) | collective-permute-done | bytes 262176 | tf_op jit(solution)/shard_map/ppermute | solution.py:607
  73.1 0.6 shard_map.149
  73.7 1.1 collective-permute-start.1
  74.7 2.7 %collective-permute-start.2 = (f32[4,16,256]{2,1,0:T(8,128)S(1)}, f32[4,16,256]{2,1,0:T(8,128)S(1)}, u32[]{:S(2)}, u32[]{:S(2)}) collective-permute-start(f32[4,16,256]{2,1,0:T(8,128)S(1)} %get-tuple-element.34), channel_id=1, source_target_pairs={{0,64},{16,80},{32,96},{48,112},{64,0},{80,16},{96,32},{112,48},{1... | collective-permute-start | bytes 196616 | tf_op jit(solution)/shard_map/ppermute | solution.py:611
  77.4 1.4 %collective-permute-start.3 = (f32[4,16,256]{2,1,0:T(8,128)S(1)}, f32[4,16,256]{2,1,0:T(8,128)S(1)}, u32[]{:S(2)}, u32[]{:S(2)}) collective-permute-start(f32[4,16,256]{2,1,0:T(8,128)S(1)} %get-tuple-element.35), channel_id=1, source_target_pairs={{0,96},{16,112},{32,0},{48,16},{64,32},{80,48},{96,64},{112,80},{1... | collective-permute-start | bytes 196616 | tf_op jit(solution)/shard_map/ppermute | solution.py:611
  78.8 0.9 collective-permute-done.1.refs_2_
  79.7 1.6 %collective-permute-done.2.refs_3_ = f32[4,16,256]{2,1,0:T(8,128)S(1)} collective-permute-done((f32[4,16,256]{2,1,0:T(8,128)S(1)}, f32[4,16,256]{2,1,0:T(8,128)S(1)}, u32[]{:S(2)}, u32[]{:S(2)}) %collective-permute-start.2) | collective-permute-done | bytes 65568 | tf_op jit(solution)/shard_map/ppermute | solution.py:611
  81.7 0.8 shard_map.150.refs_3_
  82.4 2.7 %collective-permute-start.6 = (f32[4,16,256]{2,1,0:T(8,128)S(1)}, f32[4,16,256]{2,1,0:T(8,128)S(1)}, u32[]{:S(2)}, u32[]{:S(2)}) collective-permute-start(f32[4,16,256]{2,1,0:T(8,128)S(1)} %shard_map.150.refs_3_), channel_id=1, source_target_pairs={{0,96},{16,112},{32,0},{48,16},{64,32},{80,48},{96,64},{112,80},{1... | collective-permute-start | bytes 196616 | tf_op jit(solution)/shard_map/ppermute | solution.py:611
  86.1 1.6 %collective-permute-done.6.refs_6_ = f32[4,16,256]{2,1,0:T(8,128)S(1)} collective-permute-done((f32[4,16,256]{2,1,0:T(8,128)S(1)}, f32[4,16,256]{2,1,0:T(8,128)S(1)}, u32[]{:S(2)}, u32[]{:S(2)}) %collective-permute-start.6) | collective-permute-done | bytes 65568 | tf_op jit(solution)/shard_map/ppermute | solution.py:611
  87.6 3.3 %collective-permute-done.5.refs_5_ = f32[4,16,256]{2,1,0:T(8,128)S(1)} collective-permute-done((f32[4,16,256]{2,1,0:T(8,128)S(1)}, f32[4,16,256]{2,1,0:T(8,128)S(1)}, u32[]{:S(2)}, u32[]{:S(2)}) %collective-permute-start.5) | collective-permute-done | bytes 65568 | tf_op jit(solution)/shard_map/ppermute | solution.py:611
  90.9 0.7 collective-permute-done.4.refs_4_
  91.6 0.6 collective-permute-done.9.refs_9_
  92.2 0.7 collective-permute-done.8.refs_8_
  92.9 10.7 %shard_map.151 = f32[32,32,128]{2,1,0:T(8,128)} custom-call(s32[4]{0:T(128)S(1)} %pad_add_fusion.refs_0_, s32[16]{0:T(128)S(1)} %get-tuple-element.24.refs_1_, s32[32,128]{1,0:T(8,128)S(1)} %get-tuple-element.25.refs_2_, f32[4,16,256]{2,1,0:T(8,128)S(1)} %shard_map.150.refs_3_, f32[4,16,256]{2,1,0:T(8,128)S(1)} %collective-permute-done.4.refs_4_, ...), custom_call_target="tpu_custom_call" | custom-call | tf_op jit(solution)/shard_map/pallas_call | solution.py:581
  103.6 7.0 %all-to-all-start.2 = ((f32[32,32,128]{2,1,0:T(8,128)}), f32[32,32,128]{2,1,0:T(8,128)S(1)}, u32[]{:S(2)}, u32[]{:S(2)}) async-start(f32[32,32,128]{2,1,0:T(8,128)} %shard_map.151), calls=%async_computation.2 | async-start | bytes 1048576 | tf_op jit(solution)/shard_map/all_to_all | solution.py:603
  110.6 2.4 %shard_map.154.refs_2_ = f32[32,8192]{1,0:T(8,128)S(1)} custom-call(f32[2048,128]{1,0:T(8,128)S(1)} %bitcast.16, f32[2,32,128]{2,1,0:T(8,128)S(1)} %get-tuple-element.27.refs_6_.refs_15_.refs_1_, bf16[4,256,256]{2,1,0:T(8,128)(2,1)} %constant.49.clone.refs_16_.refs_2_), custom_call_target="tpu_custom_call" | custom-call | tf_op jit(solution)/shard_map/pallas_call | solution.py:581
  113.0 9.5 %all-to-all-done.2.refs_1_ = f32[32,32,128]{2,1,0:T(8,128)S(1)} async-done(((f32[32,32,128]{2,1,0:T(8,128)}), f32[32,32,128]{2,1,0:T(8,128)S(1)}, u32[]{:S(2)}, u32[]{:S(2)}) %all-to-all-start.2) | async-done | bytes 524320 | tf_op jit(solution)/shard_map/all_to_all | solution.py:603
  122.5 2.1 %shard_map.155 = f32[32,8192]{1,0:T(8,128)} custom-call(s32[16,128]{1,0:T(8,128)S(1)} %bitcast.18, f32[32,32,128]{2,1,0:T(8,128)S(1)} %all-to-all-done.2.refs_1_, f32[32,8192]{1,0:T(8,128)S(1)} %shard_map.154.refs_2_), custom_call_target="tpu_custom_call" | custom-call | tf_op jit(solution)/shard_map/pallas_call | solution.py:581
  (12 shorter events, 1.5 us)
Async XLA Ops:
  1.4 15.6 %all-to-all-start = ((s32[16,1,128]{2,1,0:T(1,128)}), s32[16,1,128]{2,1,0:T(1,128)S(1)}, u32[]{:S(2)}, u32[]{:S(2)}) async-start(s32[16,1,128]{2,1,0:T(1,128)} %bitcast.2), calls=%async_computation | async-start | bytes 16384 | tf_op jit(solution)/shard_map/all_to_all | solution.py:603
  17.0 25.4 %all-to-all-start.3 = ((f32[128,16,128]{2,1,0:T(8,128)}), f32[128,16,128]{2,1,0:T(8,128)S(1)}, u32[]{:S(2)}, u32[]{:S(2)}) async-start(f32[128,16,128]{2,1,0:T(8,128)} %bitcast.12), calls=%async_computation.3 | async-start | bytes 2097152 | tf_op jit(solution)/shard_map/all_to_all | solution.py:603
  42.4 15.3 %all-to-all-start.1 = ((f32[32,32,128]{2,1,0:T(8,128)}), f32[32,32,128]{2,1,0:T(8,128)S(1)}, u32[]{:S(2)}, u32[]{:S(2)}) async-start(f32[32,32,128]{2,1,0:T(8,128)} %shard_map.147), calls=%async_computation.1 | async-start | bytes 1048576 | tf_op jit(solution)/shard_map/all_to_all | solution.py:603
  57.7 45.9 %all-to-all-start.4 = ((f32[128,16,128]{2,1,0:T(8,128)}), f32[128,16,128]{2,1,0:T(8,128)S(1)}, u32[]{:S(2)}, u32[]{:S(2)}) async-start(f32[128,16,128]{2,1,0:T(8,128)} %shard_map.153), calls=%async_computation.4 | async-start | bytes 2097152 | tf_op jit(solution)/shard_map/all_to_all | solution.py:603
  71.5 1.6 %collective-permute-start = (f32[16,16,256]{2,1,0:T(8,128)S(1)}, f32[16,16,256]{2,1,0:T(8,128)S(1)}, u32[]{:S(2)}, u32[]{:S(2)}) collective-permute-start(f32[16,16,256]{2,1,0:T(8,128)S(1)} %get-tuple-element.31), channel_id=1, source_target_pairs={{0,16},{16,0},{32,48},{48,32},{64,80},{80,64},{96,112},{112,96},{1... | collective-permute-start | bytes 786440 | tf_op jit(solution)/shard_map/ppermute | solution.py:607
  73.7 6.1 %collective-permute-start.1 = (f32[4,16,256]{2,1,0:T(8,128)S(1)}, f32[4,16,256]{2,1,0:T(8,128)S(1)}, u32[]{:S(2)}, u32[]{:S(2)}) collective-permute-start(f32[4,16,256]{2,1,0:T(8,128)S(1)} %get-tuple-element.33), channel_id=1, source_target_pairs={{0,32},{16,48},{32,64},{48,80},{64,96},{80,112},{96,0},{112,16},{1... | collective-permute-start | bytes 196616 | tf_op jit(solution)/shard_map/ppermute | solution.py:611
  74.7 6.6 %collective-permute-start.2 = (f32[4,16,256]{2,1,0:T(8,128)S(1)}, f32[4,16,256]{2,1,0:T(8,128)S(1)}, u32[]{:S(2)}, u32[]{:S(2)}) collective-permute-start(f32[4,16,256]{2,1,0:T(8,128)S(1)} %get-tuple-element.34), channel_id=1, source_target_pairs={{0,64},{16,80},{32,96},{48,112},{64,0},{80,16},{96,32},{112,48},{1... | collective-permute-start | bytes 196616 | tf_op jit(solution)/shard_map/ppermute | solution.py:611
  77.4 4.3 %collective-permute-start.3 = (f32[4,16,256]{2,1,0:T(8,128)S(1)}, f32[4,16,256]{2,1,0:T(8,128)S(1)}, u32[]{:S(2)}, u32[]{:S(2)}) collective-permute-start(f32[4,16,256]{2,1,0:T(8,128)S(1)} %get-tuple-element.35), channel_id=1, source_target_pairs={{0,96},{16,112},{32,0},{48,16},{64,32},{80,48},{96,64},{112,80},{1... | collective-permute-start | bytes 196616 | tf_op jit(solution)/shard_map/ppermute | solution.py:611
  82.4 5.2 %collective-permute-start.6 = (f32[4,16,256]{2,1,0:T(8,128)S(1)}, f32[4,16,256]{2,1,0:T(8,128)S(1)}, u32[]{:S(2)}, u32[]{:S(2)}) collective-permute-start(f32[4,16,256]{2,1,0:T(8,128)S(1)} %shard_map.150.refs_3_), channel_id=1, source_target_pairs={{0,96},{16,112},{32,0},{48,16},{64,32},{80,48},{96,64},{112,80},{1... | collective-permute-start | bytes 196616 | tf_op jit(solution)/shard_map/ppermute | solution.py:611
  85.1 5.8 %collective-permute-start.5 = (f32[4,16,256]{2,1,0:T(8,128)S(1)}, f32[4,16,256]{2,1,0:T(8,128)S(1)}, u32[]{:S(2)}, u32[]{:S(2)}) collective-permute-start(f32[4,16,256]{2,1,0:T(8,128)S(1)} %shard_map.150.refs_3_), channel_id=1, source_target_pairs={{0,64},{16,80},{32,96},{48,112},{64,0},{80,16},{96,32},{112,48},{1... | collective-permute-start | bytes 196616 | tf_op jit(solution)/shard_map/ppermute | solution.py:611
  85.7 5.9 %collective-permute-start.4 = (f32[4,16,256]{2,1,0:T(8,128)S(1)}, f32[4,16,256]{2,1,0:T(8,128)S(1)}, u32[]{:S(2)}, u32[]{:S(2)}) collective-permute-start(f32[4,16,256]{2,1,0:T(8,128)S(1)} %shard_map.150.refs_3_), channel_id=1, source_target_pairs={{0,32},{16,48},{32,64},{48,80},{64,96},{80,112},{96,0},{112,16},{1... | collective-permute-start | bytes 196616 | tf_op jit(solution)/shard_map/ppermute | solution.py:611
  86.1 5.5 %collective-permute-start.7 = (f32[4,16,256]{2,1,0:T(8,128)S(1)}, f32[4,16,256]{2,1,0:T(8,128)S(1)}, u32[]{:S(2)}, u32[]{:S(2)}) collective-permute-start(f32[4,16,256]{2,1,0:T(8,128)S(1)} %shard_map.150.refs_3_), channel_id=1, source_target_pairs={{0,16},{16,0},{32,48},{48,32},{64,80},{80,64},{96,112},{112,96},{1... | collective-permute-start | bytes 196616 | tf_op jit(solution)/shard_map/ppermute | solution.py:607
  87.6 4.0 %collective-permute-start.10 = (f32[4,16,256]{2,1,0:T(8,128)S(1)}, f32[4,16,256]{2,1,0:T(8,128)S(1)}, u32[]{:S(2)}, u32[]{:S(2)}) collective-permute-start(f32[4,16,256]{2,1,0:T(8,128)S(1)} %collective-permute-done.6.refs_6_), channel_id=1, source_target_pairs={{0,16},{16,0},{32,48},{48,32},{64,80},{80,64},{96,112},{112,96},{1... | collective-permute-start | bytes 196616 | tf_op jit(solution)/shard_map/ppermute | solution.py:607
  90.9 1.3 %collective-permute-start.9 = (f32[4,16,256]{2,1,0:T(8,128)S(1)}, f32[4,16,256]{2,1,0:T(8,128)S(1)}, u32[]{:S(2)}, u32[]{:S(2)}) collective-permute-start(f32[4,16,256]{2,1,0:T(8,128)S(1)} %collective-permute-done.5.refs_5_), channel_id=1, source_target_pairs={{0,16},{16,0},{32,48},{48,32},{64,80},{80,64},{96,112},{112,96},{1... | collective-permute-start | bytes 196616 | tf_op jit(solution)/shard_map/ppermute | solution.py:607
  91.6 1.3 %collective-permute-start.8 = (f32[4,16,256]{2,1,0:T(8,128)S(1)}, f32[4,16,256]{2,1,0:T(8,128)S(1)}, u32[]{:S(2)}, u32[]{:S(2)}) collective-permute-start(f32[4,16,256]{2,1,0:T(8,128)S(1)} %collective-permute-done.4.refs_4_), channel_id=1, source_target_pairs={{0,16},{16,0},{32,48},{48,32},{64,80},{80,64},{96,112},{112,96},{1... | collective-permute-start | bytes 196616 | tf_op jit(solution)/shard_map/ppermute | solution.py:607
  103.6 18.9 %all-to-all-start.2 = ((f32[32,32,128]{2,1,0:T(8,128)}), f32[32,32,128]{2,1,0:T(8,128)S(1)}, u32[]{:S(2)}, u32[]{:S(2)}) async-start(f32[32,32,128]{2,1,0:T(8,128)} %shard_map.151), calls=%async_computation.2 | async-start | bytes 1048576 | tf_op jit(solution)/shard_map/all_to_all | solution.py:603

commit v4 on v3

--- a/solution.py
+++ b/solution.py
@@ -164,7 +164,9 @@
     return pl.ds(pl.multiple_of(index * size, size), size)
 
 
-def ids_kernel(owner, block, send, slots, counts):
+def ids_kernel(owner, block, sky_hbm, send, slots, sky, counts, sem):
+    copy = pltpu.make_async_copy(sky_hbm, sky, sem)
+    copy.start()
     for i in range(16):
         counts[i] = 0
     row = lax.broadcasted_iota(jnp.int32, (16, 128), 0)
@@ -177,6 +179,7 @@
         slots[i] = target * 2 + place
         table = jnp.where((row == target) & (lane == place), block[i], table)
     send[...] = table
+    copy.wait()
 
 
 def pick_kernel(asked, sky, out, sem):
@@ -632,21 +635,21 @@
     flat = (32, 32, 128)
     loading_t, inv_white = mode_loading.T, inv_white.T
 
-    send, slots = call(
+    send, slots, sky_v = call(
         ids_kernel,
-        "tt",
-        (request_owner.reshape(16), request_block),
-        [((16, 128), jnp.int32), ((16,), jnp.int32)],
-        [SM((16,), jnp.int32)],
-        [VM, SM],
+        "tth",
+        (request_owner.reshape(16), request_block, sky_map),
+        [((16, 128), jnp.int32), ((16,), jnp.int32), ((32, 8192), F32)],
+        [SM((16,), jnp.int32), DMA],
+        [VM, SM, KEEP],
     )
     asked = exchange(send, "tm")
-    outgoing = call(pick_kernel, "sh", (asked, sky_map), [(flat, F32)], [DMA((32,))])
+    outgoing = call(pick_kernel, "sw", (asked, sky_v), [(flat, F32)], [DMA((32,))], [HBM])
     arrived = exchange(outgoing, "tm")
 
     wide = ((2048, 128), F32)
     packed = call(
-        rows_kernel, "eel", (sky_map, turn, ahead), [wide], [half, VM((1024, 256), F32)]
+        rows_kernel, "wel", (sky_v, turn, ahead), [wide], [half, VM((1024, 256), F32)]
     )
     columns = exchange(packed.reshape(128, 16, 128), ("det", "tm"))
 

time: 125 us -> 126 us (level)
  waiting for transfers between devices: 43.9 us -> 45.8 us
    all_to_all x5, waiting for transfers between devices: 32.7 us -> 34.7 us  [exchange(): return lax.all_to_all(value, axes, split_axis=0, concat_axis=0, tiled=True)]
  transfers between devices with their start and end apart: 16 -> 16, of which waited for: 13 -> 13; matrix products, arithmetic and copies ran while one was open for 0% -> 0% of each run, Pallas kernels for 31% -> 29%
where the time goes in v4:
time: 126 us
  waiting for transfers between devices  45.8 us (36%)
  Pallas kernels  41.1 us (33%)
  starting transfers between devices  38.6 us (31%)
    pallas_call x11, Pallas kernels, call(): result = run(*ins)  41.1 us
    all_to_all x5, waiting for transfers between devices, exchange(): return lax.all_to_all(value, axes, split_axis=0, concat_axis=0, tiled=True)  34.7 us
    all_to_all x5, starting transfers between devices, exchange(): return lax.all_to_all(value, axes, split_axis=0, concat_axis=0, tiled=True)  29.7 us
    ppermute x6, starting transfers between devices, chip_shift(): lax.ppermute(value, 'det', [(g, (g + 2 * step) % 8) for g in range(8)])  8.8 us
    ppermute x6, waiting for transfers between devices, chip_shift(): lax.ppermute(value, 'det', [(g, (g + 2 * step) % 8) for g in range(8)])  8.36 us
    ppermute x5, waiting for transfers between devices, core_swap(): return lax.ppermute(value, 'det', [(g, g ^ 1) for g in range(8)])  2.77 us
  transfers between devices with their start and end apart: 16, of which 13 were waited for; matrix products, arithmetic and copies ran while one was open for 0% of the time, Pallas kernels for 29%

profile of v4, /device:TPU:0, one launch (start us, length us, event | category | flops | bytes accessed | tf_op | source)
XLA Modules:
  0.0 125.8 jit_solution(17366981885687845952)
XLA Ops:
  0.0 2.5 %shard_map.145 = (s32[16,128]{1,0:T(8,128)}, s32[16]{0:T(128)S(1)}, f32[32,8192]{1,0:T(8,128)S(1)}) custom-call(s32[16]{0:T(128)} %bitcast.23, s32[16]{0:T(128)} %refs_1_.3, f32[32,8192]{1,0:T(8,128)} %refs_2_.4), custom_call_target="tpu_custom_call" | custom-call | tf_op jit(solution)/shard_map/pallas_call | solution.py:584
  2.5 8.0 %all-to-all-start = ((s32[16,1,128]{2,1,0:T(1,128)}), s32[16,1,128]{2,1,0:T(1,128)S(1)}, u32[]{:S(2)}, u32[]{:S(2)}) async-start(s32[16,1,128]{2,1,0:T(1,128)} %bitcast.2), calls=%async_computation | async-start | bytes 16384 | tf_op jit(solution)/shard_map/all_to_all | solution.py:606
  10.5 3.1 %shard_map.152 = f32[2048,128]{1,0:T(8,128)} custom-call(f32[32,8192]{1,0:T(8,128)S(1)} %get-tuple-element.27.refs_1_.refs_0_, f32[2,32,128]{2,1,0:T(8,128)} %constant.47.clone.refs_5_.refs_1_, bf16[4,256,256]{2,1,0:T(8,128)(2,1)} %constant.48.clone.refs_6_.refs_2_), custom_call_target="tpu_custom_call" | custom-call | tf_op jit(solution)/shard_map/pallas_call | solution.py:584
  13.6 4.5 %all-to-all-done = s32[16,1,128]{2,1,0:T(1,128)S(1)} async-done(((s32[16,1,128]{2,1,0:T(1,128)}), s32[16,1,128]{2,1,0:T(1,128)S(1)}, u32[]{:S(2)}, u32[]{:S(2)}) %all-to-all-start) | async-done | bytes 8224 | tf_op jit(solution)/shard_map/all_to_all | solution.py:606
  18.1 6.4 %all-to-all-start.3 = ((f32[128,16,128]{2,1,0:T(8,128)}), f32[128,16,128]{2,1,0:T(8,128)S(1)}, u32[]{:S(2)}, u32[]{:S(2)}) async-start(f32[128,16,128]{2,1,0:T(8,128)} %bitcast.12), calls=%async_computation.3 | async-start | bytes 2097152 | tf_op jit(solution)/shard_map/all_to_all | solution.py:606
  24.5 1.8 %shard_map.147 = f32[32,32,128]{2,1,0:T(8,128)} custom-call(s32[16,128]{1,0:T(8,128)S(1)} %bitcast.17, f32[32,8192]{1,0:T(8,128)S(1)} %get-tuple-element.27.refs_1_.refs_0_), custom_call_target="tpu_custom_call" | custom-call | tf_op jit(solution)/shard_map/pallas_call | solution.py:584
  26.3 17.2 %all-to-all-done.3.refs_1_ = f32[128,16,128]{2,1,0:T(8,128)S(1)} async-done(((f32[128,16,128]{2,1,0:T(8,128)}), f32[128,16,128]{2,1,0:T(8,128)S(1)}, u32[]{:S(2)}, u32[]{:S(2)}) %all-to-all-start.3) | async-done | bytes 1048608 | tf_op jit(solution)/shard_map/all_to_all | solution.py:606
  43.5 3.6 %all-to-all-start.1 = ((f32[32,32,128]{2,1,0:T(8,128)}), f32[32,32,128]{2,1,0:T(8,128)S(1)}, u32[]{:S(2)}, u32[]{:S(2)}) async-start(f32[32,32,128]{2,1,0:T(8,128)} %shard_map.147), calls=%async_computation.1 | async-start | bytes 1048576 | tf_op jit(solution)/shard_map/all_to_all | solution.py:606
  47.1 2.8 %shard_map.146 = (f32[2,32,128]{2,1,0:T(8,128)S(1)}, bf16[4,256,256]{2,1,0:T(8,128)(2,1)S(1)}, f32[128,128]{1,0:T(8,128)S(1)}, f32[2,64,128]{2,1,0:T(8,128)S(1)}...) custom-call(f32[32,64]{1,0:T(8,128)} %bitcast.22, ...), custom_call_target="tpu_custom_call" | custom-call | tf_op jit(solution)/shard_map/pallas_call | solution.py:584
  50.0 5.4 %shard_map.153 = f32[128,16,128]{2,1,0:T(8,128)} custom-call(s32[4]{0:T(128)S(1)} %pad_add_fusion.refs_0_, f32[128,16,128]{2,1,0:T(8,128)S(1)} %all-to-all-done.3.refs_1_, f32[2,64,128]{2,1,0:T(8,128)S(1)} %get-tuple-element.41.refs_2_, bf16[8,256,256]{2,1,0:T(8,128)(2,1)S(1)} %get-tuple-element.42.refs_3_), custom_call_target="tpu_custom_call" | custom-call | tf_op jit(solution)/shard_map/pallas_call | solution.py:584
  55.4 3.5 %all-to-all-done.1.refs_4_ = f32[32,32,128]{2,1,0:T(8,128)S(1)} async-done(((f32[32,32,128]{2,1,0:T(8,128)}), f32[32,32,128]{2,1,0:T(8,128)S(1)}, u32[]{:S(2)}, u32[]{:S(2)}) %all-to-all-start.1) | async-done | bytes 524320 | tf_op jit(solution)/shard_map/all_to_all | solution.py:606
  58.8 4.8 %all-to-all-start.4 = ((f32[128,16,128]{2,1,0:T(8,128)}), f32[128,16,128]{2,1,0:T(8,128)S(1)}, u32[]{:S(2)}, u32[]{:S(2)}) async-start(f32[128,16,128]{2,1,0:T(8,128)} %shard_map.153), calls=%async_computation.4 | async-start | bytes 2097152 | tf_op jit(solution)/shard_map/all_to_all | solution.py:606
  63.6 9.0 %shard_map.148 = (f32[32,64,256]{2,1,0:T(8,128)}, f32[16,16,256]{2,1,0:T(8,128)S(1)}, f32[16,16,256]{2,1,0:T(8,128)S(1)}) custom-call(s32[4]{0:T(128)S(1)} %pad_add_fusion.refs_0_, s32[16]{0:T(128)S(1)} %get-tuple-element.25.refs_1_, s32[64,64]{1,0:T(8,128)} %refs_2_.5, f32[64,8192]{1,0:T(8,128)} %refs_3_.1, f32[32,32,128]{2,1,0:T(8,128)S(1)} %all-to-all-done.1.refs_4_, ...), custom_call_target="tpu_custom_call" | custom-call | tf_op jit(solution)/shard_map/pallas_call | solution.py:584
  72.7 1.5 %collective-permute-done.refs_2_ = f32[16,16,256]{2,1,0:T(8,128)S(1)} collective-permute-done((f32[16,16,256]{2,1,0:T(8,128)S(1)}, f32[16,16,256]{2,1,0:T(8,128)S(1)}, u32[]{:S(2)}, u32[]{:S(2)}) %collective-permute-start) | collective-permute-done | bytes 262176 | tf_op jit(solution)/shard_map/ppermute | solution.py:610
  74.2 0.6 shard_map.149
  74.8 1.0 collective-permute-start.1
  75.8 2.8 %collective-permute-start.2 = (f32[4,16,256]{2,1,0:T(8,128)S(1)}, f32[4,16,256]{2,1,0:T(8,128)S(1)}, u32[]{:S(2)}, u32[]{:S(2)}) collective-permute-start(f32[4,16,256]{2,1,0:T(8,128)S(1)} %get-tuple-element.36), channel_id=1, source_target_pairs={{0,64},{16,80},{32,96},{48,112},{64,0},{80,16},{96,32},{112,48},{1... | collective-permute-start | bytes 196616 | tf_op jit(solution)/shard_map/ppermute | solution.py:614
  78.5 1.4 %collective-permute-start.3 = (f32[4,16,256]{2,1,0:T(8,128)S(1)}, f32[4,16,256]{2,1,0:T(8,128)S(1)}, u32[]{:S(2)}, u32[]{:S(2)}) collective-permute-start(f32[4,16,256]{2,1,0:T(8,128)S(1)} %get-tuple-element.37), channel_id=1, source_target_pairs={{0,96},{16,112},{32,0},{48,16},{64,32},{80,48},{96,64},{112,80},{1... | collective-permute-start | bytes 196616 | tf_op jit(solution)/shard_map/ppermute | solution.py:614
  80.0 0.9 collective-permute-done.1.refs_2_
  80.8 1.6 %collective-permute-done.2.refs_3_ = f32[4,16,256]{2,1,0:T(8,128)S(1)} collective-permute-done((f32[4,16,256]{2,1,0:T(8,128)S(1)}, f32[4,16,256]{2,1,0:T(8,128)S(1)}, u32[]{:S(2)}, u32[]{:S(2)}) %collective-permute-start.2) | collective-permute-done | bytes 65568 | tf_op jit(solution)/shard_map/ppermute | solution.py:614
  82.8 0.8 shard_map.150.refs_3_
  83.6 2.7 %collective-permute-start.6 = (f32[4,16,256]{2,1,0:T(8,128)S(1)}, f32[4,16,256]{2,1,0:T(8,128)S(1)}, u32[]{:S(2)}, u32[]{:S(2)}) collective-permute-start(f32[4,16,256]{2,1,0:T(8,128)S(1)} %shard_map.150.refs_3_), channel_id=1, source_target_pairs={{0,96},{16,112},{32,0},{48,16},{64,32},{80,48},{96,64},{112,80},{1... | collective-permute-start | bytes 196616 | tf_op jit(solution)/shard_map/ppermute | solution.py:614
  87.2 1.6 %collective-permute-done.6.refs_6_ = f32[4,16,256]{2,1,0:T(8,128)S(1)} collective-permute-done((f32[4,16,256]{2,1,0:T(8,128)S(1)}, f32[4,16,256]{2,1,0:T(8,128)S(1)}, u32[]{:S(2)}, u32[]{:S(2)}) %collective-permute-start.6) | collective-permute-done | bytes 65568 | tf_op jit(solution)/shard_map/ppermute | solution.py:614
  88.8 3.3 %collective-permute-done.5.refs_5_ = f32[4,16,256]{2,1,0:T(8,128)S(1)} collective-permute-done((f32[4,16,256]{2,1,0:T(8,128)S(1)}, f32[4,16,256]{2,1,0:T(8,128)S(1)}, u32[]{:S(2)}, u32[]{:S(2)}) %collective-permute-start.5) | collective-permute-done | bytes 65568 | tf_op jit(solution)/shard_map/ppermute | solution.py:614
  92.1 0.7 collective-permute-done.4.refs_4_
  92.7 0.6 collective-permute-done.9.refs_9_
  93.3 0.7 collective-permute-done.8.refs_8_
  94.0 10.7 %shard_map.151 = f32[32,32,128]{2,1,0:T(8,128)} custom-call(s32[4]{0:T(128)S(1)} %pad_add_fusion.refs_0_, s32[16]{0:T(128)S(1)} %get-tuple-element.25.refs_1_, s32[32,128]{1,0:T(8,128)S(1)} %get-tuple-element.26.refs_2_, f32[4,16,256]{2,1,0:T(8,128)S(1)} %shard_map.150.refs_3_, f32[4,16,256]{2,1,0:T(8,128)S(1)} %collective-permute-done.4.refs_4_, ...), custom_call_target="tpu_custom_call" | custom-call | tf_op jit(solution)/shard_map/pallas_call | solution.py:584
  104.7 7.0 %all-to-all-start.2 = ((f32[32,32,128]{2,1,0:T(8,128)}), f32[32,32,128]{2,1,0:T(8,128)S(1)}, u32[]{:S(2)}, u32[]{:S(2)}) async-start(f32[32,32,128]{2,1,0:T(8,128)} %shard_map.151), calls=%async_computation.2 | async-start | bytes 1048576 | tf_op jit(solution)/shard_map/all_to_all | solution.py:606
  111.8 2.4 %shard_map.154.refs_2_ = f32[32,8192]{1,0:T(8,128)S(1)} custom-call(f32[2048,128]{1,0:T(8,128)S(1)} %bitcast.16, f32[2,32,128]{2,1,0:T(8,128)S(1)} %get-tuple-element.29.refs_6_.refs_15_.refs_1_, bf16[4,256,256]{2,1,0:T(8,128)(2,1)} %constant.49.clone.refs_16_.refs_2_), custom_call_target="tpu_custom_call" | custom-call | tf_op jit(solution)/shard_map/pallas_call | solution.py:584
  114.2 9.5 %all-to-all-done.2.refs_1_ = f32[32,32,128]{2,1,0:T(8,128)S(1)} async-done(((f32[32,32,128]{2,1,0:T(8,128)}), f32[32,32,128]{2,1,0:T(8,128)S(1)}, u32[]{:S(2)}, u32[]{:S(2)}) %all-to-all-start.2) | async-done | bytes 524320 | tf_op jit(solution)/shard_map/all_to_all | solution.py:606
  123.7 2.1 %shard_map.155 = f32[32,8192]{1,0:T(8,128)} custom-call(s32[16,128]{1,0:T(8,128)S(1)} %bitcast.18, f32[32,32,128]{2,1,0:T(8,128)S(1)} %all-to-all-done.2.refs_1_, f32[32,8192]{1,0:T(8,128)S(1)} %shard_map.154.refs_2_), custom_call_target="tpu_custom_call" | custom-call | tf_op jit(solution)/shard_map/pallas_call | solution.py:584
  (12 shorter events, 1.5 us)
Async XLA Ops:
  2.5 15.6 %all-to-all-start = ((s32[16,1,128]{2,1,0:T(1,128)}), s32[16,1,128]{2,1,0:T(1,128)S(1)}, u32[]{:S(2)}, u32[]{:S(2)}) async-start(s32[16,1,128]{2,1,0:T(1,128)} %bitcast.2), calls=%async_computation | async-start | bytes 16384 | tf_op jit(solution)/shard_map/all_to_all | solution.py:606
  18.1 25.4 %all-to-all-start.3 = ((f32[128,16,128]{2,1,0:T(8,128)}), f32[128,16,128]{2,1,0:T(8,128)S(1)}, u32[]{:S(2)}, u32[]{:S(2)}) async-start(f32[128,16,128]{2,1,0:T(8,128)} %bitcast.12), calls=%async_computation.3 | async-start | bytes 2097152 | tf_op jit(solution)/shard_map/all_to_all | solution.py:606
  43.5 15.3 %all-to-all-start.1 = ((f32[32,32,128]{2,1,0:T(8,128)}), f32[32,32,128]{2,1,0:T(8,128)S(1)}, u32[]{:S(2)}, u32[]{:S(2)}) async-start(f32[32,32,128]{2,1,0:T(8,128)} %shard_map.147), calls=%async_computation.1 | async-start | bytes 1048576 | tf_op jit(solution)/shard_map/all_to_all | solution.py:606
  58.8 45.9 %all-to-all-start.4 = ((f32[128,16,128]{2,1,0:T(8,128)}), f32[128,16,128]{2,1,0:T(8,128)S(1)}, u32[]{:S(2)}, u32[]{:S(2)}) async-start(f32[128,16,128]{2,1,0:T(8,128)} %shard_map.153), calls=%async_computation.4 | async-start | bytes 2097152 | tf_op jit(solution)/shard_map/all_to_all | solution.py:606
  72.6 1.6 %collective-permute-start = (f32[16,16,256]{2,1,0:T(8,128)S(1)}, f32[16,16,256]{2,1,0:T(8,128)S(1)}, u32[]{:S(2)}, u32[]{:S(2)}) collective-permute-start(f32[16,16,256]{2,1,0:T(8,128)S(1)} %get-tuple-element.33), channel_id=1, source_target_pairs={{0,16},{16,0},{32,48},{48,32},{64,80},{80,64},{96,112},{112,96},{1... | collective-permute-start | bytes 786440 | tf_op jit(solution)/shard_map/ppermute | solution.py:610
  74.8 6.0 %collective-permute-start.1 = (f32[4,16,256]{2,1,0:T(8,128)S(1)}, f32[4,16,256]{2,1,0:T(8,128)S(1)}, u32[]{:S(2)}, u32[]{:S(2)}) collective-permute-start(f32[4,16,256]{2,1,0:T(8,128)S(1)} %get-tuple-element.35), channel_id=1, source_target_pairs={{0,32},{16,48},{32,64},{48,80},{64,96},{80,112},{96,0},{112,16},{1... | collective-permute-start | bytes 196616 | tf_op jit(solution)/shard_map/ppermute | solution.py:614
  75.8 6.7 %collective-permute-start.2 = (f32[4,16,256]{2,1,0:T(8,128)S(1)}, f32[4,16,256]{2,1,0:T(8,128)S(1)}, u32[]{:S(2)}, u32[]{:S(2)}) collective-permute-start(f32[4,16,256]{2,1,0:T(8,128)S(1)} %get-tuple-element.36), channel_id=1, source_target_pairs={{0,64},{16,80},{32,96},{48,112},{64,0},{80,16},{96,32},{112,48},{1... | collective-permute-start | bytes 196616 | tf_op jit(solution)/shard_map/ppermute | solution.py:614
  78.5 4.3 %collective-permute-start.3 = (f32[4,16,256]{2,1,0:T(8,128)S(1)}, f32[4,16,256]{2,1,0:T(8,128)S(1)}, u32[]{:S(2)}, u32[]{:S(2)}) collective-permute-start(f32[4,16,256]{2,1,0:T(8,128)S(1)} %get-tuple-element.37), channel_id=1, source_target_pairs={{0,96},{16,112},{32,0},{48,16},{64,32},{80,48},{96,64},{112,80},{1... | collective-permute-start | bytes 196616 | tf_op jit(solution)/shard_map/ppermute | solution.py:614
  83.6 5.2 %collective-permute-start.6 = (f32[4,16,256]{2,1,0:T(8,128)S(1)}, f32[4,16,256]{2,1,0:T(8,128)S(1)}, u32[]{:S(2)}, u32[]{:S(2)}) collective-permute-start(f32[4,16,256]{2,1,0:T(8,128)S(1)} %shard_map.150.refs_3_), channel_id=1, source_target_pairs={{0,96},{16,112},{32,0},{48,16},{64,32},{80,48},{96,64},{112,80},{1... | collective-permute-start | bytes 196616 | tf_op jit(solution)/shard_map/ppermute | solution.py:614
  86.3 5.8 %collective-permute-start.5 = (f32[4,16,256]{2,1,0:T(8,128)S(1)}, f32[4,16,256]{2,1,0:T(8,128)S(1)}, u32[]{:S(2)}, u32[]{:S(2)}) collective-permute-start(f32[4,16,256]{2,1,0:T(8,128)S(1)} %shard_map.150.refs_3_), channel_id=1, source_target_pairs={{0,64},{16,80},{32,96},{48,112},{64,0},{80,16},{96,32},{112,48},{1... | collective-permute-start | bytes 196616 | tf_op jit(solution)/shard_map/ppermute | solution.py:614
  86.8 5.9 %collective-permute-start.4 = (f32[4,16,256]{2,1,0:T(8,128)S(1)}, f32[4,16,256]{2,1,0:T(8,128)S(1)}, u32[]{:S(2)}, u32[]{:S(2)}) collective-permute-start(f32[4,16,256]{2,1,0:T(8,128)S(1)} %shard_map.150.refs_3_), channel_id=1, source_target_pairs={{0,32},{16,48},{32,64},{48,80},{64,96},{80,112},{96,0},{112,16},{1... | collective-permute-start | bytes 196616 | tf_op jit(solution)/shard_map/ppermute | solution.py:614
  87.2 5.5 %collective-permute-start.7 = (f32[4,16,256]{2,1,0:T(8,128)S(1)}, f32[4,16,256]{2,1,0:T(8,128)S(1)}, u32[]{:S(2)}, u32[]{:S(2)}) collective-permute-start(f32[4,16,256]{2,1,0:T(8,128)S(1)} %shard_map.150.refs_3_), channel_id=1, source_target_pairs={{0,16},{16,0},{32,48},{48,32},{64,80},{80,64},{96,112},{112,96},{1... | collective-permute-start | bytes 196616 | tf_op jit(solution)/shard_map/ppermute | solution.py:610
  88.8 4.0 %collective-permute-start.10 = (f32[4,16,256]{2,1,0:T(8,128)S(1)}, f32[4,16,256]{2,1,0:T(8,128)S(1)}, u32[]{:S(2)}, u32[]{:S(2)}) collective-permute-start(f32[4,16,256]{2,1,0:T(8,128)S(1)} %collective-permute-done.6.refs_6_), channel_id=1, source_target_pairs={{0,16},{16,0},{32,48},{48,32},{64,80},{80,64},{96,112},{112,96},{1... | collective-permute-start | bytes 196616 | tf_op jit(solution)/shard_map/ppermute | solution.py:610
  92.1 1.3 collective-permute-start.9
  92.7 1.3 collective-permute-start.8
  104.7 18.9 %all-to-all-start.2 = ((f32[32,32,128]{2,1,0:T(8,128)}), f32[32,32,128]{2,1,0:T(8,128)S(1)}, u32[]{:S(2)}, u32[]{:S(2)}) async-start(f32[32,32,128]{2,1,0:T(8,128)} %shard_map.151), calls=%async_computation.2 | async-start | bytes 1048576 | tf_op jit(solution)/shard_map/all_to_all | solution.py:606
